TPU v7x, 32 devices: a whole 2x2x4 slice. The times are simulated.
32 devices in a mesh: days: 2 (over y), chan: 8 (over z, x), win: 2 (over core).
Axes of the slice: x: 2, y: 2, z: 4, core: 2. Of those that a mesh axis runs over, the one named last changes fastest.
Arguments:
- records: bfloat16 [2048, 2, 3000], P(('days', 'chan'), 'win'), parts along dimension 0, may hold values from -6 to 6
- assign: int32 [1024], P('chan'), may hold values from 0 to 127, as said below
- plan: int32 [1], replicated, may hold values from 0 to 2
- seg_mask: int32 [16, 2], P(('days', 'chan'), 'win'), parts along dimension 0, may hold values 0 or 1
Outputs:
- correlations: float32 [2, 1024, 128, 64], P('days', 'chan', 'win'), parts along dimension 0
There are 2 independent parts, one for each index of `days`. A program takes and returns all parts, laid end to end along the dimension named above; an argument that names none is the same for every part. Nothing has to cross between parts.
Inputs may be any that keep to these rules, and one draw needn't show every extreme that they name: `assign`: each aligned group of 128 entries holds every number from 0 to 127 once.
All inputs are finite; a program needn't handle non-finite values. No bound on the sum of `seg_mask` on one device may be relied on, other than what follows from the above.
Results may differ from a plain program's by a relative error of at most 0.005.
Values may be sent and summed in bfloat16 or wider, within the bound.
No kernel may reach another device: no remote copies, remote signals or barrier semaphores. Data moves between devices by JAX's collectives and lax.ppermute only.
A program may use at most 64 MiB of HBM per device.

v0:
```python
import math

import jax
import jax.numpy as jnp
from jax import lax
from jax.experimental import pallas as pl
from jax.experimental.pallas import tpu as pltpu
from jax.sharding import PartitionSpec as P


LAGS = 64
HALF = LAGS // 2
GROUP = 16
NEARS = 2
LOADS = 1
FARS = (16, 16, 16, 16)
BF16 = jnp.bfloat16
F32 = jnp.float32
PARAMS = pltpu.CompilerParams(vmem_limit_bytes=24 * 1024 * 1024)

NEAR_PARAMS = pltpu.CompilerParams(vmem_limit_bytes=62 * 1024 * 1024)
SMEM = pl.BlockSpec(memory_space=pltpu.SMEM)
VMEM = pl.BlockSpec(memory_space=pltpu.VMEM)
ANY = pl.BlockSpec(memory_space=pl.ANY)
HBM = pl.BlockSpec(memory_space=pltpu.HBM)


def store_turned(rows, pad_ref, start, size, out_refs):
    turned = lax.dot_general(
        rows, pad_ref[pl.ds(start, size), :], (((1,), (1,)), ((), ())), preferred_element_type=F32
    )
    at = 0
    for out_ref in out_refs:
        count = out_ref.shape[0]
        out_ref[:, pl.ds(start, size)] = turned[at : at + count].astype(BF16)
        at += count


def near_body(win_ref, rec_ref, assign_ref, near_ref, pad_ref, rows_ref, pick_ref, turn_ref, slot_ref, sem):
    seg_len, chans = rec_ref.shape
    width = pad_ref.shape[0]
    half = chans // 2
    tail = width - HALF - seg_len
    slots = pltpu.make_async_copy(assign_ref, slot_ref, sem.at[LOADS])
    slots.start()
    step = width // LOADS
    loads = []
    for at in range(LOADS):
        low = max(at * step - HALF, 0)
        count = min((at + 1) * step - HALF, seg_len) - low
        target = pad_ref.at[pl.ds(HALF + low, count)]
        loads.append(pltpu.make_async_copy(rec_ref.at[pl.ds(low, count)], target, sem.at[at]))
        loads[-1].start()
    pad_ref[pl.ds(0, HALF), :] = jnp.zeros((HALF, chans), BF16)
    pad_ref[pl.ds(HALF + seg_len, tail), :] = jnp.zeros((tail, chans), BF16)
    slots.wait()
    source = lax.broadcasted_iota(jnp.int32, (chans, chans), 0)
    pick = jnp.where(source == slot_ref[...], 1.0, 0.0)
    pick_ref[...] = pick.astype(BF16)
    turn_ref[...] = pick.T
    near = pl.multiple_of(win_ref[0] * half, half)
    far = pl.multiple_of((1 - win_ref[0]) * half, half)
    count = near_ref.shape[0]
    rest = half - count
    rows_ref[pl.ds(0, rest), :] = turn_ref[pl.ds(near + count, rest), :].astype(BF16)
    rows_ref[pl.ds(rest, half), :] = turn_ref[pl.ds(far, half), :].astype(BF16)
    rows = turn_ref[pl.ds(near, count), :].astype(BF16)
    for at in range(LOADS):
        loads[at].wait()
        store_turned(rows, pad_ref, at * step, step, (near_ref,))


def rest_body(mask_ref, pad_ref, rows_ref, pick_ref, own_ref, meta_ref, *out_refs):
    width, chans = pad_ref.shape
    mask = mask_ref[0, 0].astype(F32)
    meta_ref[...] = jnp.full(meta_ref.shape, mask, F32)
    store_turned(rows_ref[...], pad_ref, 0, width, out_refs)
    for out_ref in out_refs:
        ending = out_ref[:, pl.ds(width - 128, 128)].astype(F32)
        last = lax.broadcasted_iota(jnp.int32, ending.shape, 1) == 127
        out_ref[:, pl.ds(width - 128, 128)] = jnp.where(last, mask, ending).astype(BF16)
    ordered = jnp.dot(pad_ref[...], pick_ref[...], preferred_element_type=F32)
    own_ref[pl.ds(0, width), :] = ordered.astype(BF16)
    own_ref[pl.ds(width, HALF), :] = jnp.zeros((HALF, chans), BF16)
    own_ref[pl.ds(width + HALF, 16), :] = jnp.full((16, chans), mask, F32).astype(BF16)


def correlate(part, own_ref, lhs_ref):
    count, width = part.shape
    pack = GROUP // count
    if pack == 2:
        part = jnp.concatenate([part, pltpu.roll(part, width - 1, 1)], axis=0)
    for lag in range(0, HALF, pack):
        moved = part if lag == 0 else pltpu.roll(part, width - lag, 1)
        lhs_ref[pl.ds(lag * count, GROUP), :] = moved
    rhs = jnp.concatenate([own_ref[pl.ds(HALF, width), :], own_ref[pl.ds(0, width), :]], axis=1)
    return jnp.dot(lhs_ref[...], rhs, preferred_element_type=F32)


def first_body(own_ref, part_ref, *refs):
    term_ref, lhs_ref = refs[-2:]

    def step(at, carry):
        part = part_ref[pl.ds(pl.multiple_of(at * GROUP, GROUP), GROUP), :]
        terms = correlate(part, own_ref, lhs_ref).astype(BF16)
        term_ref[pl.ds(pl.multiple_of(at * GROUP * HALF, GROUP), GROUP * HALF), :] = terms
        return carry

    lax.fori_loop(0, part_ref.shape[0] // GROUP, step, 0)


def second_body(before, row, skip, final, seg_len, meta_ref, own_ref, part_ref, mark_ref, term_ref, *refs):
    lhs_ref, sem = refs[-2:]
    count, width = part_ref.shape
    chans = own_ref.shape[1]
    outs = []
    if before:
        prior_ref = refs[0]
        out_ref = refs[2] if row > before else refs[1]
        target = out_ref.at[pl.ds((row - before) * LAGS, before * LAGS)]
        outs.append(pltpu.make_async_copy(prior_ref, target, sem.at[0]))
        outs[-1].start()
    done_ref = refs[-3]
    ending = pl.ds(width - 128, 128)
    here = meta_ref[pl.ds(0, count), :] * mark_ref[pl.ds(0, count), ending].astype(F32)
    there = own_ref[pl.ds(width + HALF, count), :].astype(F32) * part_ref[:, ending].astype(F32)
    here = here[:, 127:128]
    there = there[:, 127:128]
    scale = 1.0 / (jnp.maximum(here + there, 1.0) * math.sqrt(seg_len))
    here = jnp.broadcast_to(here * scale, (count, chans))
    there = jnp.broadcast_to(there * scale, (count, chans))
    terms = correlate(part_ref[...], own_ref, lhs_ref).astype(BF16).astype(F32)
    slab = 8
    for low in range(0, count, slab):
        at = skip + low
        held_at = at // GROUP * GROUP * HALF + at % GROUP
        for lag in range(HALF):
            for high in range(2):
                lanes = pl.ds(high * chans, chans)
                line = lag * count + low
                mine = terms[line : line + slab, high * chans : (high + 1) * chans]
                held = term_ref[pl.ds(held_at + lag * GROUP, slab), lanes].astype(F32)
                total = mine * there[low : low + slab] + held * here[low : low + slab]
                done_ref[pl.ds(low * LAGS + high * HALF + lag, slab, stride=LAGS), :] = total
        if final:
            source = done_ref.at[pl.ds(low * LAGS, slab * LAGS)]
            target = out_ref.at[pl.ds((row + low) * LAGS, slab * LAGS)]
            outs.append(pltpu.make_async_copy(source, target, sem.at[1 + low // slab]))
            outs[-1].start()
    for out in outs:
        out.wait()


def body(records, assign, plan, seg_mask):
    chans, seg_count, seg_len = records.shape
    blocks = lax.axis_size("chan")
    half = chans // lax.axis_size("win")
    width = -(-(seg_len + LAGS) // 256) * 256
    win = lax.axis_index("win").astype(jnp.int32).reshape(1)
    rec = records.reshape(chans, seg_count * seg_len).T
    slots = assign.reshape(1, chans)
    per_near = half // NEARS
    shape = jax.ShapeDtypeStruct
    near_prep = pl.pallas_call(
        near_body,
        out_shape=(
            shape((per_near, width), BF16),
            shape((width, chans), BF16),
            shape((2 * half - per_near, chans), BF16),
            shape((chans, chans), BF16),
        ),
        in_specs=[SMEM, HBM, HBM],
        out_specs=(VMEM,) * 4,
        scratch_shapes=[
            pltpu.VMEM((chans, chans), F32),
            pltpu.VMEM((1, chans), jnp.int32),
            pltpu.SemaphoreType.DMA((LOADS + 1,)),
        ],
        compiler_params=NEAR_PARAMS,
        cost_estimate=pl.CostEstimate(flops=1 << 26, bytes_accessed=1 << 20, transcendentals=0),
        name="near_prep",
    )
    counts = (per_near,) * (NEARS - 1) + FARS
    rest_prep = pl.pallas_call(
        rest_body,
        out_shape=(shape((width + HALF + 16, chans), BF16), shape((16, 128), F32))
        + tuple(shape((count, width), BF16) for count in counts),
        in_specs=[SMEM] + [VMEM] * 3,
        out_specs=(VMEM,) * (len(counts) + 2),
        compiler_params=PARAMS,
        cost_estimate=pl.CostEstimate(flops=1 << 27, bytes_accessed=1 << 20, transcendentals=0),
        name="rest_prep",
    )
    rows = GROUP * HALF
    flops = 2 * rows * width * 2 * chans
    lhs = pltpu.VMEM((rows, width), BF16)

    def first(*args):
        return pl.pallas_call(
            first_body,
            out_shape=shape((per_near * HALF, 2 * chans), BF16),
            in_specs=[VMEM, VMEM] + [ANY] * (len(args) - 2),
            out_specs=VMEM,
            scratch_shapes=[lhs],
            compiler_params=PARAMS,
            cost_estimate=pl.CostEstimate(flops=2 * flops, bytes_accessed=1 << 20, transcendentals=0),
            name="first",
        )(*args)

    def second(before, row, count):
        skip = row % per_near
        final = row + count == half
        total = shape((half * LAGS, chans), F32)
        done = shape((count * LAGS, chans), F32)
        lines = pltpu.VMEM((count * HALF, width), BF16)
        sems = pltpu.SemaphoreType.DMA((3,))
        if final:
            extra = dict(out_shape=(total,), out_specs=(ANY,))
            scratch = [pltpu.VMEM(done.shape, F32), lines, sems]
        elif before:
            extra = dict(out_shape=(total, done), out_specs=(ANY, VMEM))
            scratch = [lines, sems]
        else:
            extra = dict(out_shape=(done,), out_specs=(VMEM,))
            scratch = [lines, sems]
        return pl.pallas_call(
            lambda *refs: second_body(before, row, skip, final, seg_len, *refs),
            in_specs=[VMEM] * 5 + [VMEM] * (before > 0) + [ANY] * (row > before),
            scratch_shapes=scratch,
            input_output_aliases={6: 0} if row > before else {},
            compiler_params=PARAMS,
            cost_estimate=pl.CostEstimate(flops=flops, bytes_accessed=1 << 20, transcendentals=0),
            name="second",
            **extra,
        )

    def exchange(bit):
        straight = []
        crossed = []
        for low in range(blocks):
            for core in range(2):
                straight.append((low * 2 + core, (low ^ 1 << bit) * 2 + core))
                crossed.append((low * 2 + core, (low ^ 1 << bit) * 2 + 1 - core))

        def run(near0, pad, turned, pick, flags):
            own, meta, *pieces = rest_prep(flags, pad, turned, pick)
            near = []
            for one in [near0] + pieces[: NEARS - 1]:
                near.append(lax.ppermute(one, ("chan", "win"), straight))
            far = []
            for one in pieces[NEARS - 1 :]:
                far.append(lax.ppermute(one, ("chan", "win"), crossed))
            other = lax.ppermute(own, "win", [(0, 1), (1, 0)])
            terms = []
            for one in near:
                terms.append(first(own, one, *terms[-1:]))
            out = done = ()
            before = row = 0
            for one in far:
                count = one.shape[0]
                side = row // per_near
                step = second(before, row, count)
                result = step(meta, other, one, near[-1], terms[side], *done, *out)
                out = result[:1] if before else ()
                done = result[-1:]
                before = count
                row += count
            return out[0]

        return run

    digits = blocks.bit_length() - 1
    held = near_prep(win, rec, slots)
    branches = [exchange(bit) for bit in range(digits)]
    out = lax.switch(plan[0], branches, *held, seg_mask)
    return jnp.transpose(out.reshape(half, LAGS, chans), (2, 0, 1))[None]


def solution(mesh):
    placed = (P(("days", "chan"), "win", None), P("chan"), P(), P(("days", "chan"), "win"))
    return jax.shard_map(
        body, mesh=mesh, in_specs=placed, out_specs=P("days", "chan", "win", None), check_vma=False
    )
```

profile of v0, /device:TPU:0, one launch (start us, length us, event | category | flops | bytes accessed | tf_op | source)
XLA Modules:
  0.0 31.9 jit_solution(10690364067944372864)
XLA Ops:
  0.7 1.5 %near_prep.1 = (bf16[32,3072]{1,0:T(8,128)(2,1)S(1)}, bf16[3072,128]{1,0:T(8,128)(2,1)S(1)}, bf16[96,128]{1,0:T(8,128)(2,1)S(1)}, bf16[128,128]{1,0:T(8,128)(2,1)S(1)}) custom-call(s32[1]{0:T(128)} %bitcast.1.win_ref, bf16[3000,128]{1,0:T(8,128)(2,1)} %bitcast.11, s32[1,128]{1,0:T(1,128)} %bitcast.12), custom_call_target="tpu_custom_call" | custom-call | flops 67108864 | bytes 1048576 | tf_op jit(solution)/shard_map/near_prep/pallas_call | solution.py:273
  2.2 29.5 %conditional.1 = (f32[4096,128]{1,0:T(8,128)}) conditional(s32[]{:T(128)} %bitcast, (s32[1,1]{1,0:T(1,128)}, bf16[3072,128]{1,0:T(8,128)(2,1)S(1)}, bf16[96,128]{1,0:T(8,128)(2,1)S(1)}, bf16[128,128]{1,0:T(8,128)(2,1)S(1)}, bf16[32,3072]{1,0:T(8,128)(2,1)S(1)}) %tuple.14, (s32[1,1]{1,0:T(1,128)}, bf16[3072,128]{1,0:T(8,128)(2,1)S(1)}, ...), branch_computations={%region_0.0_spmd, %region_1.0_spmd, %region_2.0_spmd} | conditional | flops 6576668672 | bytes 13680928 | solution.py:275
  2.2 1.2 %rest_prep.3 = (bf16[3120,128]{1,0:T(8,128)(2,1)S(1)}, f32[16,128]{1,0:T(8,128)S(1)}, bf16[32,3072]{1,0:T(8,128)(2,1)S(1)}, bf16[16,3072]{1,0:T(8,128)(2,1)S(1)}...) custom-call(s32[1,1]{1,0:T(1,128)} %get-tuple-element.38.mask_ref, ...), custom_call_target="tpu_custom_call" | custom-call | flops 134217728 | bytes 1048576 | tf_op jit(solution)/shard_map/cond/branch_0_fun/rest_prep/pallas_call | solution.py:246
  3.5 0.6 %collective-permute-start = (bf16[3120,128]{1,0:T(8,128)(2,1)S(1)}, bf16[3120,128]{1,0:T(8,128)(2,1)S(1)}, u32[]{:S(2)}, u32[]{:S(2)}) collective-permute-start(bf16[3120,128]{1,0:T(8,128)(2,1)S(1)} %get-tuple-element.44.own_ref), channel_id=1, source_target_pairs={{0,1},{1,0},{2,3},{3,2},{4,5},{5,4},{6,7},{7,6},{8,9},{9,8},{10,11... | collective-permute-start | bytes 2396168 | tf_op jit(solution)/shard_map/cond/branch_0_fun/ppermute | solution.py:253
  4.0 2.6 %collective-permute-start.3 = (bf16[32,3072]{1,0:T(8,128)(2,1)S(1)}, bf16[32,3072]{1,0:T(8,128)(2,1)S(1)}, u32[]{:S(2)}, u32[]{:S(2)}) collective-permute-start(bf16[32,3072]{1,0:T(8,128)(2,1)S(1)} %get-tuple-element.47), channel_id=1, source_target_pairs={{0,2},{1,3},{2,0},{3,1},{4,6},{5,7},{6,4},{7,5},{8,10},{9,11},{10,... | collective-permute-start | bytes 589832 | tf_op jit(solution)/shard_map/cond/branch_0_fun/ppermute | solution.py:249
  6.6 0.1 collective-permute-start.2
  6.7 1.4 %collective-permute-start.1 = (bf16[16,3072]{1,0:T(8,128)(2,1)S(1)}, bf16[16,3072]{1,0:T(8,128)(2,1)S(1)}, u32[]{:S(2)}, u32[]{:S(2)}) collective-permute-start(bf16[16,3072]{1,0:T(8,128)(2,1)S(1)} %get-tuple-element.45), channel_id=1, source_target_pairs={{0,3},{1,2},{2,1},{3,0},{4,7},{5,6},{6,5},{7,4},{8,11},{9,10},{10,... | collective-permute-start | bytes 294920 | tf_op jit(solution)/shard_map/cond/branch_0_fun/ppermute | solution.py:252
  8.1 0.3 %collective-permute-start.4 = (bf16[16,3072]{1,0:T(8,128)(2,1)S(1)}, bf16[16,3072]{1,0:T(8,128)(2,1)S(1)}, u32[]{:S(2)}, u32[]{:S(2)}) collective-permute-start(bf16[16,3072]{1,0:T(8,128)(2,1)S(1)} %get-tuple-element.48), channel_id=1, source_target_pairs={{0,3},{1,2},{2,1},{3,0},{4,7},{5,6},{6,5},{7,4},{8,11},{9,10},{10,... | collective-permute-start | bytes 294920 | tf_op jit(solution)/shard_map/cond/branch_0_fun/ppermute | solution.py:252
  8.4 3.9 %collective-permute-done.3.part_ref = bf16[32,3072]{1,0:T(8,128)(2,1)S(1)} collective-permute-done((bf16[32,3072]{1,0:T(8,128)(2,1)S(1)}, bf16[32,3072]{1,0:T(8,128)(2,1)S(1)}, u32[]{:S(2)}, u32[]{:S(2)}) %collective-permute-start.3) | collective-permute-done | bytes 196640 | tf_op jit(solution)/shard_map/cond/branch_0_fun/ppermute | solution.py:249
  12.3 0.7 %collective-permute-start.5 = (bf16[16,3072]{1,0:T(8,128)(2,1)S(1)}, bf16[16,3072]{1,0:T(8,128)(2,1)S(1)}, u32[]{:S(2)}, u32[]{:S(2)}) collective-permute-start(bf16[16,3072]{1,0:T(8,128)(2,1)S(1)} %get-tuple-element.49), channel_id=1, source_target_pairs={{0,3},{1,2},{2,1},{3,0},{4,7},{5,6},{6,5},{7,4},{8,11},{9,10},{10,... | collective-permute-start | bytes 294920 | tf_op jit(solution)/shard_map/cond/branch_0_fun/ppermute | solution.py:252
  13.0 2.2 %first.6.refs_0_.refs_4_ = bf16[1024,256]{1,0:T(8,128)(2,1)S(1)} custom-call(bf16[3120,128]{1,0:T(8,128)(2,1)S(1)} %get-tuple-element.44.own_ref, bf16[32,3072]{1,0:T(8,128)(2,1)S(1)} %collective-permute-done.3.part_ref), custom_call_target="tpu_custom_call" | custom-call | flops 1610612736 | bytes 1048576 | tf_op jit(solution)/shard_map/cond/branch_0_fun/first/pallas_call | solution.py:199
  15.2 1.4 %collective-permute-done.2.part_ref.refs_3_ = bf16[32,3072]{1,0:T(8,128)(2,1)S(1)} collective-permute-done((bf16[32,3072]{1,0:T(8,128)(2,1)S(1)}, bf16[32,3072]{1,0:T(8,128)(2,1)S(1)}, u32[]{:S(2)}, u32[]{:S(2)}) %collective-permute-start.2) | collective-permute-done | bytes 196640 | tf_op jit(solution)/shard_map/cond/branch_0_fun/ppermute | solution.py:249
  16.5 0.7 %collective-permute-start.6 = (bf16[16,3072]{1,0:T(8,128)(2,1)S(1)}, bf16[16,3072]{1,0:T(8,128)(2,1)S(1)}, u32[]{:S(2)}, u32[]{:S(2)}) collective-permute-start(bf16[16,3072]{1,0:T(8,128)(2,1)S(1)} %get-tuple-element.50), channel_id=1, source_target_pairs={{0,3},{1,2},{2,1},{3,0},{4,7},{5,6},{6,5},{7,4},{8,11},{9,10},{10,... | collective-permute-start | bytes 294920 | tf_op jit(solution)/shard_map/cond/branch_0_fun/ppermute | solution.py:252
  17.2 2.2 %first.7.refs_4_ = bf16[1024,256]{1,0:T(8,128)(2,1)S(1)} custom-call(bf16[3120,128]{1,0:T(8,128)(2,1)S(1)} %get-tuple-element.44.own_ref, bf16[32,3072]{1,0:T(8,128)(2,1)S(1)} %collective-permute-done.2.part_ref.refs_3_, bf16[1024,256]{1,0:T(8,128)(2,1)S(1)} %first.6.refs_0_.refs_4_), custom_call_target="tpu_custom_call" | custom-call | flops 1610612736 | bytes 1048576 | tf_op jit(solution)/shard_map/cond/branch_0_fun/first/pallas_call | solution.py:199
  19.4 5.1 %collective-permute-done.6.refs_2_ = bf16[16,3072]{1,0:T(8,128)(2,1)S(1)} collective-permute-done((bf16[16,3072]{1,0:T(8,128)(2,1)S(1)}, bf16[16,3072]{1,0:T(8,128)(2,1)S(1)}, u32[]{:S(2)}, u32[]{:S(2)}) %collective-permute-start.6) | collective-permute-done | bytes 98336 | tf_op jit(solution)/shard_map/cond/branch_0_fun/ppermute | solution.py:252
  24.4 0.0 collective-permute-done.refs_1_
  24.5 1.5 %second.12.refs_5_ = f32[1024,128]{1,0:T(8,128)S(1)} custom-call(f32[16,128]{1,0:T(8,128)S(1)} %get-tuple-element.43.refs_0_, bf16[3120,128]{1,0:T(8,128)(2,1)S(1)} %collective-permute-done.refs_1_, bf16[16,3072]{1,0:T(8,128)(2,1)S(1)} %collective-permute-done.6.refs_2_, bf16[32,3072]{1,0:T(8,128)(2,1)S(1)} %collective-permute-done.2.part_ref.refs_3_, ...), custom_call_target="tpu_custom_call" | custom-call | flops 805306368 | bytes 1048576 | tf_op jit(solution)/shard_map/cond/branch_0_fun/second/pallas_call | solution.py:263
  26.0 0.0 collective-permute-done.5.refs_2_
  26.0 1.6 %second.13 = (f32[4096,128]{1,0:T(8,128)}, f32[1024,128]{1,0:T(8,128)S(1)}) custom-call(f32[16,128]{1,0:T(8,128)S(1)} %get-tuple-element.43.refs_0_, bf16[3120,128]{1,0:T(8,128)(2,1)S(1)} %collective-permute-done.refs_1_, bf16[16,3072]{1,0:T(8,128)(2,1)S(1)} %collective-permute-done.5.refs_2_, bf16[32,3072]{1,0:T(8,128)(2,1)S(1)} %collective-permute-done.2.part_ref.refs_3_, ...), custom_call_target="tpu_custom_call" | custom-call | flops 805306368 | bytes 1048576 | tf_op jit(solution)/shard_map/cond/branch_0_fun/second/pallas_call | solution.py:263
  27.6 0.0 collective-permute-done.4.refs_2_
  27.6 1.6 %second.14 = (f32[4096,128]{1,0:T(8,128)}, f32[1024,128]{1,0:T(8,128)S(1)}) custom-call(f32[16,128]{1,0:T(8,128)S(1)} %get-tuple-element.43.refs_0_, bf16[3120,128]{1,0:T(8,128)(2,1)S(1)} %collective-permute-done.refs_1_, bf16[16,3072]{1,0:T(8,128)(2,1)S(1)} %collective-permute-done.4.refs_2_, ...), custom_call_target="tpu_custom_call", output_to_operand_aliasing={{0}: (6, {})} | custom-call | flops 805306368 | bytes 1048576 | tf_op jit(solution)/shard_map/cond/branch_0_fun/second/pallas_call | solution.py:263
  29.3 0.0 collective-permute-done.1.refs_2_
  29.3 2.2 %second.15 = f32[4096,128]{1,0:T(8,128)} custom-call(f32[16,128]{1,0:T(8,128)S(1)} %get-tuple-element.43.refs_0_, bf16[3120,128]{1,0:T(8,128)(2,1)S(1)} %collective-permute-done.refs_1_, bf16[16,3072]{1,0:T(8,128)(2,1)S(1)} %collective-permute-done.1.refs_2_, ...), custom_call_target="tpu_custom_call", output_to_operand_aliasing={{}: (6, {})} | custom-call | flops 805306368 | bytes 1048576 | tf_op jit(solution)/shard_map/cond/branch_0_fun/second/pallas_call | solution.py:263
Async XLA Ops:
  3.5 21.0 %collective-permute-start = (bf16[3120,128]{1,0:T(8,128)(2,1)S(1)}, bf16[3120,128]{1,0:T(8,128)(2,1)S(1)}, u32[]{:S(2)}, u32[]{:S(2)}) collective-permute-start(bf16[3120,128]{1,0:T(8,128)(2,1)S(1)} %get-tuple-element.44.own_ref), channel_id=1, source_target_pairs={{0,1},{1,0},{2,3},{3,2},{4,5},{5,4},{6,7},{7,6},{8,9},{9,8},{10,11... | collective-permute-start | bytes 2396168 | tf_op jit(solution)/shard_map/cond/branch_0_fun/ppermute | solution.py:253
  4.0 8.3 %collective-permute-start.3 = (bf16[32,3072]{1,0:T(8,128)(2,1)S(1)}, bf16[32,3072]{1,0:T(8,128)(2,1)S(1)}, u32[]{:S(2)}, u32[]{:S(2)}) collective-permute-start(bf16[32,3072]{1,0:T(8,128)(2,1)S(1)} %get-tuple-element.47), channel_id=1, source_target_pairs={{0,2},{1,3},{2,0},{3,1},{4,6},{5,7},{6,4},{7,5},{8,10},{9,11},{10,... | collective-permute-start | bytes 589832 | tf_op jit(solution)/shard_map/cond/branch_0_fun/ppermute | solution.py:249
  6.6 10.0 %collective-permute-start.2 = (bf16[32,3072]{1,0:T(8,128)(2,1)S(1)}, bf16[32,3072]{1,0:T(8,128)(2,1)S(1)}, u32[]{:S(2)}, u32[]{:S(2)}) collective-permute-start(bf16[32,3072]{1,0:T(8,128)(2,1)S(1)} %get-tuple-element.46), channel_id=1, source_target_pairs={{0,2},{1,3},{2,0},{3,1},{4,6},{5,7},{6,4},{7,5},{8,10},{9,11},{10,... | collective-permute-start | bytes 589832 | tf_op jit(solution)/shard_map/cond/branch_0_fun/ppermute | solution.py:249
  6.7 22.6 %collective-permute-start.1 = (bf16[16,3072]{1,0:T(8,128)(2,1)S(1)}, bf16[16,3072]{1,0:T(8,128)(2,1)S(1)}, u32[]{:S(2)}, u32[]{:S(2)}) collective-permute-start(bf16[16,3072]{1,0:T(8,128)(2,1)S(1)} %get-tuple-element.45), channel_id=1, source_target_pairs={{0,3},{1,2},{2,1},{3,0},{4,7},{5,6},{6,5},{7,4},{8,11},{9,10},{10,... | collective-permute-start | bytes 294920 | tf_op jit(solution)/shard_map/cond/branch_0_fun/ppermute | solution.py:252
  8.1 19.5 %collective-permute-start.4 = (bf16[16,3072]{1,0:T(8,128)(2,1)S(1)}, bf16[16,3072]{1,0:T(8,128)(2,1)S(1)}, u32[]{:S(2)}, u32[]{:S(2)}) collective-permute-start(bf16[16,3072]{1,0:T(8,128)(2,1)S(1)} %get-tuple-element.48), channel_id=1, source_target_pairs={{0,3},{1,2},{2,1},{3,0},{4,7},{5,6},{6,5},{7,4},{8,11},{9,10},{10,... | collective-permute-start | bytes 294920 | tf_op jit(solution)/shard_map/cond/branch_0_fun/ppermute | solution.py:252
  12.3 13.6 %collective-permute-start.5 = (bf16[16,3072]{1,0:T(8,128)(2,1)S(1)}, bf16[16,3072]{1,0:T(8,128)(2,1)S(1)}, u32[]{:S(2)}, u32[]{:S(2)}) collective-permute-start(bf16[16,3072]{1,0:T(8,128)(2,1)S(1)} %get-tuple-element.49), channel_id=1, source_target_pairs={{0,3},{1,2},{2,1},{3,0},{4,7},{5,6},{6,5},{7,4},{8,11},{9,10},{10,... | collective-permute-start | bytes 294920 | tf_op jit(solution)/shard_map/cond/branch_0_fun/ppermute | solution.py:252
  16.5 7.9 %collective-permute-start.6 = (bf16[16,3072]{1,0:T(8,128)(2,1)S(1)}, bf16[16,3072]{1,0:T(8,128)(2,1)S(1)}, u32[]{:S(2)}, u32[]{:S(2)}) collective-permute-start(bf16[16,3072]{1,0:T(8,128)(2,1)S(1)} %get-tuple-element.50), channel_id=1, source_target_pairs={{0,3},{1,2},{2,1},{3,0},{4,7},{5,6},{6,5},{7,4},{8,11},{9,10},{10,... | collective-permute-start | bytes 294920 | tf_op jit(solution)/shard_map/cond/branch_0_fun/ppermute | solution.py:252
where the time goes:
time: 32.1 us; the launch traced here: 31.9 us
  Pallas kernels  14.1 us (44%)
  waiting for transfers between devices  10.4 us (32%)
  starting transfers between devices  6.26 us (20%)
  between operations  0.86 us (3%)
  loops' own time  0.36 us (1%)
    pallas_call x4, Pallas kernels, run(): result = step(meta, other, one, near[-1], terms[side], *done, *out)  6.94 us
    ppermute x2, waiting for transfers between devices, run(): near.append(lax.ppermute(one, ('chan', 'win'), straight))  5.3 us
    ppermute x4, waiting for transfers between devices, run(): far.append(lax.ppermute(one, ('chan', 'win'), crossed))  5.08 us
    pallas_call x2, Pallas kernels, first(): pl.pallas_call(first_body, out_shape=shape((per_near * HALF, 2 * chans),...  4.33 us
    ppermute x4, starting transfers between devices, run(): far.append(lax.ppermute(one, ('chan', 'win'), crossed))  3.07 us
    ppermute x2, starting transfers between devices, run(): near.append(lax.ppermute(one, ('chan', 'win'), straight))  2.63 us
    pallas_call x1, Pallas kernels, body(): held = near_prep(win, rec, slots)  1.53 us
    pallas_call x1, Pallas kernels, run(): own, meta, *pieces = rest_prep(flags, pad, turned, pick)  1.25 us
  transfers between devices with their start and end apart: 7, of which 3 were waited for; matrix products, arithmetic and copies ran while one was open for 0% of the time, Pallas kernels for 29%

commit v1 on v0

--- a/solution.py
+++ b/solution.py
@@ -110,7 +110,7 @@
 
 
 def second_body(before, row, skip, final, seg_len, meta_ref, own_ref, part_ref, mark_ref, term_ref, *refs):
-    lhs_ref, sem = refs[-2:]
+    lhs_ref, sem, gate = refs[-3:]
     count, width = part_ref.shape
     chans = own_ref.shape[1]
     outs = []
@@ -120,7 +120,9 @@
         target = out_ref.at[pl.ds((row - before) * LAGS, before * LAGS)]
         outs.append(pltpu.make_async_copy(prior_ref, target, sem.at[0]))
         outs[-1].start()
-    done_ref = refs[-3]
+        pl.semaphore_signal(gate, 1)
+        pl.semaphore_wait(gate, 1)
+    done_ref = refs[-4]
     ending = pl.ds(width - 128, 128)
     here = meta_ref[pl.ds(0, count), :] * mark_ref[pl.ds(0, count), ending].astype(F32)
     there = own_ref[pl.ds(width + HALF, count), :].astype(F32) * part_ref[:, ending].astype(F32)
@@ -134,14 +136,19 @@
     for low in range(0, count, slab):
         at = skip + low
         held_at = at // GROUP * GROUP * HALF + at % GROUP
-        for lag in range(HALF):
-            for high in range(2):
-                lanes = pl.ds(high * chans, chans)
-                line = lag * count + low
-                mine = terms[line : line + slab, high * chans : (high + 1) * chans]
-                held = term_ref[pl.ds(held_at + lag * GROUP, slab), lanes].astype(F32)
-                total = mine * there[low : low + slab] + held * here[low : low + slab]
-                done_ref[pl.ds(low * LAGS + high * HALF + lag, slab, stride=LAGS), :] = total
+        for high in range(2):
+            lanes = pl.ds(high * chans, chans)
+            for first in range(0, HALF, 8):
+                tiles = []
+                for lag in range(first, first + 8):
+                    line = lag * count + low
+                    mine = terms[line : line + slab, high * chans : (high + 1) * chans]
+                    held = term_ref[pl.ds(held_at + lag * GROUP, slab), lanes].astype(F32)
+                    tiles.append(mine * there[low : low + slab] + held * here[low : low + slab])
+                turned = jnp.transpose(jnp.stack(tiles, 0), (1, 0, 2))
+                for one in range(slab):
+                    spot = (low + one) * LAGS + high * HALF + first
+                    done_ref[pl.ds(spot, 8), :] = turned[one]
         if final:
             source = done_ref.at[pl.ds(low * LAGS, slab * LAGS)]
             target = out_ref.at[pl.ds((row + low) * LAGS, slab * LAGS)]
@@ -214,15 +221,16 @@
         done = shape((count * LAGS, chans), F32)
         lines = pltpu.VMEM((count * HALF, width), BF16)
         sems = pltpu.SemaphoreType.DMA((3,))
+        gate = pltpu.SemaphoreType.REGULAR
         if final:
             extra = dict(out_shape=(total,), out_specs=(ANY,))
-            scratch = [pltpu.VMEM(done.shape, F32), lines, sems]
+            scratch = [pltpu.VMEM(done.shape, F32), lines, sems, gate]
         elif before:
             extra = dict(out_shape=(total, done), out_specs=(ANY, VMEM))
-            scratch = [lines, sems]
+            scratch = [lines, sems, gate]
         else:
             extra = dict(out_shape=(done,), out_specs=(VMEM,))
-            scratch = [lines, sems]
+            scratch = [lines, sems, gate]
         return pl.pallas_call(
             lambda *refs: second_body(before, row, skip, final, seg_len, *refs),
             in_specs=[VMEM] * 5 + [VMEM] * (before > 0) + [ANY] * (row > before),

time: 32.1 us -> 30.7 us (0.956)
  Pallas kernels: 14.1 us -> 12.7 us
    pallas_call x4, Pallas kernels: 6.94 us -> 5.61 us  [run(): result = step(meta, other, one, near[-1], terms[side], *done, *out)]
  transfers between devices with their start and end apart: 7 -> 7, of which waited for: 3 -> 3; matrix products, arithmetic and copies ran while one was open for 0% -> 0% of each run, Pallas kernels for 29% -> 26%
where the time goes in v1:
time: 30.7 us; the launch traced here: 30.6 us
  Pallas kernels  12.7 us (41%)
  waiting for transfers between devices  10.4 us (34%)
  starting transfers between devices  6.26 us (20%)
  between operations  0.86 us (3%)
  loops' own time  0.36 us (1%)
    pallas_call x4, Pallas kernels, run(): result = step(meta, other, one, near[-1], terms[side], *done, *out)  5.61 us
    ppermute x2, waiting for transfers between devices, run(): near.append(lax.ppermute(one, ('chan', 'win'), straight))  5.3 us
    ppermute x4, waiting for transfers between devices, run(): far.append(lax.ppermute(one, ('chan', 'win'), crossed))  5.08 us
    pallas_call x2, Pallas kernels, first(): pl.pallas_call(first_body, out_shape=shape((per_near * HALF, 2 * chans),...  4.33 us
    ppermute x4, starting transfers between devices, run(): far.append(lax.ppermute(one, ('chan', 'win'), crossed))  3.07 us
    ppermute x2, starting transfers between devices, run(): near.append(lax.ppermute(one, ('chan', 'win'), straight))  2.63 us
    pallas_call x1, Pallas kernels, body(): held = near_prep(win, rec, slots)  1.53 us
    pallas_call x1, Pallas kernels, run(): own, meta, *pieces = rest_prep(flags, pad, turned, pick)  1.25 us
  transfers between devices with their start and end apart: 7, of which 3 were waited for; matrix products, arithmetic and copies ran while one was open for 0% of the time, Pallas kernels for 26%

profile of v1, /device:TPU:0, one launch (start us, length us, event | category | flops | bytes accessed | tf_op | source)
XLA Modules:
  0.0 30.6 jit_solution(17377371136524935832)
XLA Ops:
  0.7 1.5 %near_prep.1 = (bf16[32,3072]{1,0:T(8,128)(2,1)S(1)}, bf16[3072,128]{1,0:T(8,128)(2,1)S(1)}, bf16[96,128]{1,0:T(8,128)(2,1)S(1)}, bf16[128,128]{1,0:T(8,128)(2,1)S(1)}) custom-call(s32[1]{0:T(128)} %bitcast.1.win_ref, bf16[3000,128]{1,0:T(8,128)(2,1)} %bitcast.11, s32[1,128]{1,0:T(1,128)} %bitcast.12), custom_call_target="tpu_custom_call" | custom-call | flops 67108864 | bytes 1048576 | tf_op jit(solution)/shard_map/near_prep/pallas_call | solution.py:281
  2.2 28.2 %conditional.1 = (f32[4096,128]{1,0:T(8,128)}) conditional(s32[]{:T(128)} %bitcast, (s32[1,1]{1,0:T(1,128)}, bf16[3072,128]{1,0:T(8,128)(2,1)S(1)}, bf16[96,128]{1,0:T(8,128)(2,1)S(1)}, bf16[128,128]{1,0:T(8,128)(2,1)S(1)}, bf16[32,3072]{1,0:T(8,128)(2,1)S(1)}) %tuple.14, (s32[1,1]{1,0:T(1,128)}, bf16[3072,128]{1,0:T(8,128)(2,1)S(1)}, ...), branch_computations={%region_0.0_spmd, %region_1.0_spmd, %region_2.0_spmd} | conditional | flops 6576668672 | bytes 13680928 | solution.py:283
  2.2 1.2 %rest_prep.3 = (bf16[3120,128]{1,0:T(8,128)(2,1)S(1)}, f32[16,128]{1,0:T(8,128)S(1)}, bf16[32,3072]{1,0:T(8,128)(2,1)S(1)}, bf16[16,3072]{1,0:T(8,128)(2,1)S(1)}...) custom-call(s32[1,1]{1,0:T(1,128)} %get-tuple-element.38.mask_ref, ...), custom_call_target="tpu_custom_call" | custom-call | flops 134217728 | bytes 1048576 | tf_op jit(solution)/shard_map/cond/branch_0_fun/rest_prep/pallas_call | solution.py:254
  3.5 0.6 %collective-permute-start = (bf16[3120,128]{1,0:T(8,128)(2,1)S(1)}, bf16[3120,128]{1,0:T(8,128)(2,1)S(1)}, u32[]{:S(2)}, u32[]{:S(2)}) collective-permute-start(bf16[3120,128]{1,0:T(8,128)(2,1)S(1)} %get-tuple-element.44.own_ref), channel_id=1, source_target_pairs={{0,1},{1,0},{2,3},{3,2},{4,5},{5,4},{6,7},{7,6},{8,9},{9,8},{10,11... | collective-permute-start | bytes 2396168 | tf_op jit(solution)/shard_map/cond/branch_0_fun/ppermute | solution.py:261
  4.0 2.6 %collective-permute-start.3 = (bf16[32,3072]{1,0:T(8,128)(2,1)S(1)}, bf16[32,3072]{1,0:T(8,128)(2,1)S(1)}, u32[]{:S(2)}, u32[]{:S(2)}) collective-permute-start(bf16[32,3072]{1,0:T(8,128)(2,1)S(1)} %get-tuple-element.47), channel_id=1, source_target_pairs={{0,2},{1,3},{2,0},{3,1},{4,6},{5,7},{6,4},{7,5},{8,10},{9,11},{10,... | collective-permute-start | bytes 589832 | tf_op jit(solution)/shard_map/cond/branch_0_fun/ppermute | solution.py:257
  6.6 0.1 collective-permute-start.2
  6.7 1.4 %collective-permute-start.1 = (bf16[16,3072]{1,0:T(8,128)(2,1)S(1)}, bf16[16,3072]{1,0:T(8,128)(2,1)S(1)}, u32[]{:S(2)}, u32[]{:S(2)}) collective-permute-start(bf16[16,3072]{1,0:T(8,128)(2,1)S(1)} %get-tuple-element.45), channel_id=1, source_target_pairs={{0,3},{1,2},{2,1},{3,0},{4,7},{5,6},{6,5},{7,4},{8,11},{9,10},{10,... | collective-permute-start | bytes 294920 | tf_op jit(solution)/shard_map/cond/branch_0_fun/ppermute | solution.py:260
  8.1 0.3 %collective-permute-start.4 = (bf16[16,3072]{1,0:T(8,128)(2,1)S(1)}, bf16[16,3072]{1,0:T(8,128)(2,1)S(1)}, u32[]{:S(2)}, u32[]{:S(2)}) collective-permute-start(bf16[16,3072]{1,0:T(8,128)(2,1)S(1)} %get-tuple-element.48), channel_id=1, source_target_pairs={{0,3},{1,2},{2,1},{3,0},{4,7},{5,6},{6,5},{7,4},{8,11},{9,10},{10,... | collective-permute-start | bytes 294920 | tf_op jit(solution)/shard_map/cond/branch_0_fun/ppermute | solution.py:260
  8.4 3.9 %collective-permute-done.3.part_ref = bf16[32,3072]{1,0:T(8,128)(2,1)S(1)} collective-permute-done((bf16[32,3072]{1,0:T(8,128)(2,1)S(1)}, bf16[32,3072]{1,0:T(8,128)(2,1)S(1)}, u32[]{:S(2)}, u32[]{:S(2)}) %collective-permute-start.3) | collective-permute-done | bytes 196640 | tf_op jit(solution)/shard_map/cond/branch_0_fun/ppermute | solution.py:257
  12.3 0.7 %collective-permute-start.5 = (bf16[16,3072]{1,0:T(8,128)(2,1)S(1)}, bf16[16,3072]{1,0:T(8,128)(2,1)S(1)}, u32[]{:S(2)}, u32[]{:S(2)}) collective-permute-start(bf16[16,3072]{1,0:T(8,128)(2,1)S(1)} %get-tuple-element.49), channel_id=1, source_target_pairs={{0,3},{1,2},{2,1},{3,0},{4,7},{5,6},{6,5},{7,4},{8,11},{9,10},{10,... | collective-permute-start | bytes 294920 | tf_op jit(solution)/shard_map/cond/branch_0_fun/ppermute | solution.py:260
  13.0 2.2 %first.6.refs_0_.refs_4_ = bf16[1024,256]{1,0:T(8,128)(2,1)S(1)} custom-call(bf16[3120,128]{1,0:T(8,128)(2,1)S(1)} %get-tuple-element.44.own_ref, bf16[32,3072]{1,0:T(8,128)(2,1)S(1)} %collective-permute-done.3.part_ref), custom_call_target="tpu_custom_call" | custom-call | flops 1610612736 | bytes 1048576 | tf_op jit(solution)/shard_map/cond/branch_0_fun/first/pallas_call | solution.py:206
  15.2 1.4 %collective-permute-done.2.part_ref.refs_3_ = bf16[32,3072]{1,0:T(8,128)(2,1)S(1)} collective-permute-done((bf16[32,3072]{1,0:T(8,128)(2,1)S(1)}, bf16[32,3072]{1,0:T(8,128)(2,1)S(1)}, u32[]{:S(2)}, u32[]{:S(2)}) %collective-permute-start.2) | collective-permute-done | bytes 196640 | tf_op jit(solution)/shard_map/cond/branch_0_fun/ppermute | solution.py:257
  16.5 0.7 %collective-permute-start.6 = (bf16[16,3072]{1,0:T(8,128)(2,1)S(1)}, bf16[16,3072]{1,0:T(8,128)(2,1)S(1)}, u32[]{:S(2)}, u32[]{:S(2)}) collective-permute-start(bf16[16,3072]{1,0:T(8,128)(2,1)S(1)} %get-tuple-element.50), channel_id=1, source_target_pairs={{0,3},{1,2},{2,1},{3,0},{4,7},{5,6},{6,5},{7,4},{8,11},{9,10},{10,... | collective-permute-start | bytes 294920 | tf_op jit(solution)/shard_map/cond/branch_0_fun/ppermute | solution.py:260
  17.2 2.2 %first.7.refs_4_ = bf16[1024,256]{1,0:T(8,128)(2,1)S(1)} custom-call(bf16[3120,128]{1,0:T(8,128)(2,1)S(1)} %get-tuple-element.44.own_ref, bf16[32,3072]{1,0:T(8,128)(2,1)S(1)} %collective-permute-done.2.part_ref.refs_3_, bf16[1024,256]{1,0:T(8,128)(2,1)S(1)} %first.6.refs_0_.refs_4_), custom_call_target="tpu_custom_call" | custom-call | flops 1610612736 | bytes 1048576 | tf_op jit(solution)/shard_map/cond/branch_0_fun/first/pallas_call | solution.py:206
  19.4 5.1 %collective-permute-done.6.refs_2_ = bf16[16,3072]{1,0:T(8,128)(2,1)S(1)} collective-permute-done((bf16[16,3072]{1,0:T(8,128)(2,1)S(1)}, bf16[16,3072]{1,0:T(8,128)(2,1)S(1)}, u32[]{:S(2)}, u32[]{:S(2)}) %collective-permute-start.6) | collective-permute-done | bytes 98336 | tf_op jit(solution)/shard_map/cond/branch_0_fun/ppermute | solution.py:260
  24.4 0.0 collective-permute-done.refs_1_
  24.5 1.2 %second.12.refs_5_ = f32[1024,128]{1,0:T(8,128)S(1)} custom-call(f32[16,128]{1,0:T(8,128)S(1)} %get-tuple-element.43.refs_0_, bf16[3120,128]{1,0:T(8,128)(2,1)S(1)} %collective-permute-done.refs_1_, bf16[16,3072]{1,0:T(8,128)(2,1)S(1)} %collective-permute-done.6.refs_2_, bf16[32,3072]{1,0:T(8,128)(2,1)S(1)} %collective-permute-done.2.part_ref.refs_3_, ...), custom_call_target="tpu_custom_call" | custom-call | flops 805306368 | bytes 1048576 | tf_op jit(solution)/shard_map/cond/branch_0_fun/second/pallas_call | solution.py:271
  25.7 0.0 collective-permute-done.5.refs_2_
  25.7 1.2 %second.13 = (f32[4096,128]{1,0:T(8,128)}, f32[1024,128]{1,0:T(8,128)S(1)}) custom-call(f32[16,128]{1,0:T(8,128)S(1)} %get-tuple-element.43.refs_0_, bf16[3120,128]{1,0:T(8,128)(2,1)S(1)} %collective-permute-done.refs_1_, bf16[16,3072]{1,0:T(8,128)(2,1)S(1)} %collective-permute-done.5.refs_2_, bf16[32,3072]{1,0:T(8,128)(2,1)S(1)} %collective-permute-done.2.part_ref.refs_3_, ...), custom_call_target="tpu_custom_call" | custom-call | flops 805306368 | bytes 1048576 | tf_op jit(solution)/shard_map/cond/branch_0_fun/second/pallas_call | solution.py:271
  26.9 0.0 collective-permute-done.4.refs_2_
  26.9 1.2 %second.14 = (f32[4096,128]{1,0:T(8,128)}, f32[1024,128]{1,0:T(8,128)S(1)}) custom-call(f32[16,128]{1,0:T(8,128)S(1)} %get-tuple-element.43.refs_0_, bf16[3120,128]{1,0:T(8,128)(2,1)S(1)} %collective-permute-done.refs_1_, bf16[16,3072]{1,0:T(8,128)(2,1)S(1)} %collective-permute-done.4.refs_2_, ...), custom_call_target="tpu_custom_call", output_to_operand_aliasing={{0}: (6, {})} | custom-call | flops 805306368 | bytes 1048576 | tf_op jit(solution)/shard_map/cond/branch_0_fun/second/pallas_call | solution.py:271
  28.1 0.0 collective-permute-done.1.refs_2_
  28.1 2.0 %second.15 = f32[4096,128]{1,0:T(8,128)} custom-call(f32[16,128]{1,0:T(8,128)S(1)} %get-tuple-element.43.refs_0_, bf16[3120,128]{1,0:T(8,128)(2,1)S(1)} %collective-permute-done.refs_1_, bf16[16,3072]{1,0:T(8,128)(2,1)S(1)} %collective-permute-done.1.refs_2_, ...), custom_call_target="tpu_custom_call", output_to_operand_aliasing={{}: (6, {})} | custom-call | flops 805306368 | bytes 1048576 | tf_op jit(solution)/shard_map/cond/branch_0_fun/second/pallas_call | solution.py:271
Async XLA Ops:
  3.5 21.0 %collective-permute-start = (bf16[3120,128]{1,0:T(8,128)(2,1)S(1)}, bf16[3120,128]{1,0:T(8,128)(2,1)S(1)}, u32[]{:S(2)}, u32[]{:S(2)}) collective-permute-start(bf16[3120,128]{1,0:T(8,128)(2,1)S(1)} %get-tuple-element.44.own_ref), channel_id=1, source_target_pairs={{0,1},{1,0},{2,3},{3,2},{4,5},{5,4},{6,7},{7,6},{8,9},{9,8},{10,11... | collective-permute-start | bytes 2396168 | tf_op jit(solution)/shard_map/cond/branch_0_fun/ppermute | solution.py:261
  4.0 8.3 %collective-permute-start.3 = (bf16[32,3072]{1,0:T(8,128)(2,1)S(1)}, bf16[32,3072]{1,0:T(8,128)(2,1)S(1)}, u32[]{:S(2)}, u32[]{:S(2)}) collective-permute-start(bf16[32,3072]{1,0:T(8,128)(2,1)S(1)} %get-tuple-element.47), channel_id=1, source_target_pairs={{0,2},{1,3},{2,0},{3,1},{4,6},{5,7},{6,4},{7,5},{8,10},{9,11},{10,... | collective-permute-start | bytes 589832 | tf_op jit(solution)/shard_map/cond/branch_0_fun/ppermute | solution.py:257
  6.6 10.0 %collective-permute-start.2 = (bf16[32,3072]{1,0:T(8,128)(2,1)S(1)}, bf16[32,3072]{1,0:T(8,128)(2,1)S(1)}, u32[]{:S(2)}, u32[]{:S(2)}) collective-permute-start(bf16[32,3072]{1,0:T(8,128)(2,1)S(1)} %get-tuple-element.46), channel_id=1, source_target_pairs={{0,2},{1,3},{2,0},{3,1},{4,6},{5,7},{6,4},{7,5},{8,10},{9,11},{10,... | collective-permute-start | bytes 589832 | tf_op jit(solution)/shard_map/cond/branch_0_fun/ppermute | solution.py:257
  6.7 21.5 %collective-permute-start.1 = (bf16[16,3072]{1,0:T(8,128)(2,1)S(1)}, bf16[16,3072]{1,0:T(8,128)(2,1)S(1)}, u32[]{:S(2)}, u32[]{:S(2)}) collective-permute-start(bf16[16,3072]{1,0:T(8,128)(2,1)S(1)} %get-tuple-element.45), channel_id=1, source_target_pairs={{0,3},{1,2},{2,1},{3,0},{4,7},{5,6},{6,5},{7,4},{8,11},{9,10},{10,... | collective-permute-start | bytes 294920 | tf_op jit(solution)/shard_map/cond/branch_0_fun/ppermute | solution.py:260
  8.1 18.8 %collective-permute-start.4 = (bf16[16,3072]{1,0:T(8,128)(2,1)S(1)}, bf16[16,3072]{1,0:T(8,128)(2,1)S(1)}, u32[]{:S(2)}, u32[]{:S(2)}) collective-permute-start(bf16[16,3072]{1,0:T(8,128)(2,1)S(1)} %get-tuple-element.48), channel_id=1, source_target_pairs={{0,3},{1,2},{2,1},{3,0},{4,7},{5,6},{6,5},{7,4},{8,11},{9,10},{10,... | collective-permute-start | bytes 294920 | tf_op jit(solution)/shard_map/cond/branch_0_fun/ppermute | solution.py:260
  12.3 13.3 %collective-permute-start.5 = (bf16[16,3072]{1,0:T(8,128)(2,1)S(1)}, bf16[16,3072]{1,0:T(8,128)(2,1)S(1)}, u32[]{:S(2)}, u32[]{:S(2)}) collective-permute-start(bf16[16,3072]{1,0:T(8,128)(2,1)S(1)} %get-tuple-element.49), channel_id=1, source_target_pairs={{0,3},{1,2},{2,1},{3,0},{4,7},{5,6},{6,5},{7,4},{8,11},{9,10},{10,... | collective-permute-start | bytes 294920 | tf_op jit(solution)/shard_map/cond/branch_0_fun/ppermute | solution.py:260
  16.5 7.9 %collective-permute-start.6 = (bf16[16,3072]{1,0:T(8,128)(2,1)S(1)}, bf16[16,3072]{1,0:T(8,128)(2,1)S(1)}, u32[]{:S(2)}, u32[]{:S(2)}) collective-permute-start(bf16[16,3072]{1,0:T(8,128)(2,1)S(1)} %get-tuple-element.50), channel_id=1, source_target_pairs={{0,3},{1,2},{2,1},{3,0},{4,7},{5,6},{6,5},{7,4},{8,11},{9,10},{10,... | collective-permute-start | bytes 294920 | tf_op jit(solution)/shard_map/cond/branch_0_fun/ppermute | solution.py:260

commit v2 on v1

v2 whole, which is shorter than its diff:
```python
import math

import jax
import jax.numpy as jnp
from jax import lax
from jax.experimental import pallas as pl
from jax.experimental.pallas import tpu as pltpu
from jax.sharding import PartitionSpec as P


LAGS = 64
HALF = LAGS // 2
GROUP = 16
ORDER = (('near', 32), ('near', 32), ('far', 16), ('far', 16), ('far', 16), ('far', 16))
BF16 = jnp.bfloat16
F32 = jnp.float32
PARAMS = pltpu.CompilerParams(vmem_limit_bytes=24 * 1024 * 1024)

NEAR_PARAMS = pltpu.CompilerParams(vmem_limit_bytes=62 * 1024 * 1024)
SMEM = pl.BlockSpec(memory_space=pltpu.SMEM)
VMEM = pl.BlockSpec(memory_space=pltpu.VMEM)
ANY = pl.BlockSpec(memory_space=pl.ANY)
HBM = pl.BlockSpec(memory_space=pltpu.HBM)


def turn(rows, times_ref):
    return lax.dot_general(
        rows, times_ref[...], (((1,), (1,)), ((), ())), preferred_element_type=F32
    ).astype(BF16)


def near_body(win_ref, rec_ref, assign_ref, head_ref, pad_ref, rows_ref, pick_ref, turn_ref, slot_ref, sem):
    chans = rec_ref.shape[1]
    half = chans // 2
    count = pad_ref.shape[0] - HALF
    slots = pltpu.make_async_copy(assign_ref, slot_ref, sem.at[0])
    load = pltpu.make_async_copy(rec_ref.at[pl.ds(0, count)], pad_ref.at[pl.ds(HALF, count)], sem.at[1])
    slots.start()
    load.start()
    pad_ref[pl.ds(0, HALF), :] = jnp.zeros((HALF, chans), BF16)
    slots.wait()
    source = lax.broadcasted_iota(jnp.int32, (chans, chans), 0)
    pick = jnp.where(source == slot_ref[...], 1.0, 0.0)
    pick_ref[...] = pick.astype(BF16)
    turn_ref[...] = pick.T
    near = pl.multiple_of(win_ref[0] * half, half)
    far = pl.multiple_of((1 - win_ref[0]) * half, half)
    rows = turn_ref[pl.ds(near, half), :].astype(BF16)
    rows_ref[pl.ds(0, half), :] = rows
    rows_ref[pl.ds(half, half), :] = turn_ref[pl.ds(far, half), :].astype(BF16)
    load.wait()
    head_ref[...] = turn(rows, pad_ref)


def rest_body(nears, mask_ref, rec_ref, pad_ref, rows_ref, pick_ref, own_ref, meta_ref, *refs):
    out_refs = refs[:-2]
    tail_ref, sem = refs[-2:]
    seg_len, chans = rec_ref.shape
    head = pad_ref.shape[0]
    rest = tail_ref.shape[0]
    half = chans // 2
    count = seg_len + HALF - head
    load = pltpu.make_async_copy(
        rec_ref.at[pl.ds(head - HALF, count)], tail_ref.at[pl.ds(0, count)], sem.at[0]
    )
    load.start()
    tail_ref[pl.ds(count, rest - count), :] = jnp.zeros((rest - count, chans), BF16)
    mask = mask_ref[0, 0].astype(F32)
    meta_ref[...] = jnp.full(meta_ref.shape, mask, F32)
    early = turn(rows_ref[pl.ds(half, half), :], pad_ref)
    at = 0
    for out_ref in out_refs[nears:]:
        out_ref[:, pl.ds(0, head)] = early[at : at + out_ref.shape[0]]
        at += out_ref.shape[0]
    own_ref[pl.ds(0, head), :] = jnp.dot(
        pad_ref[...], pick_ref[...], preferred_element_type=F32
    ).astype(BF16)
    own_ref[pl.ds(head + rest, HALF), :] = jnp.zeros((HALF, chans), BF16)
    own_ref[pl.ds(head + rest + HALF, 16), :] = jnp.full((16, chans), mask, F32).astype(BF16)
    load.wait()
    late = turn(rows_ref[...], tail_ref)
    last = lax.broadcasted_iota(jnp.int32, (chans, 128), 1) == 127
    ending = jnp.where(last, mask, late[:, rest - 128 :].astype(F32)).astype(BF16)
    at = 0
    for out_ref in out_refs:
        count, width = out_ref.shape
        out_ref[:, pl.ds(width - rest, rest - 128)] = late[at : at + count, : rest - 128]
        out_ref[:, pl.ds(width - 128, 128)] = ending[at : at + count]
        at += count
    own_ref[pl.ds(head, rest), :] = jnp.dot(
        tail_ref[...], pick_ref[...], preferred_element_type=F32
    ).astype(BF16)


def correlate(part, own_ref, lhs_ref):
    count, width = part.shape
    pack = GROUP // count
    if pack == 2:
        part = jnp.concatenate([part, pltpu.roll(part, width - 1, 1)], axis=0)
    for lag in range(0, HALF, pack):
        moved = part if lag == 0 else pltpu.roll(part, width - lag, 1)
        lhs_ref[pl.ds(lag * count, GROUP), :] = moved
    rhs = jnp.concatenate([own_ref[pl.ds(HALF, width), :], own_ref[pl.ds(0, width), :]], axis=1)
    return jnp.dot(lhs_ref[...], rhs, preferred_element_type=F32)


def first_body(row, own_ref, head_ref, part_ref, *refs):
    term_ref, lhs_ref = refs[-2:]

    def step(at, carry):
        early = head_ref[pl.ds(pl.multiple_of(row + at * GROUP, GROUP), GROUP), :]
        late = part_ref[pl.ds(pl.multiple_of(at * GROUP, GROUP), GROUP), :]
        terms = correlate(jnp.concatenate([early, late], axis=1), own_ref, lhs_ref).astype(BF16)
        term_ref[pl.ds(pl.multiple_of(at * GROUP * HALF, GROUP), GROUP * HALF), :] = terms
        return carry

    lax.fori_loop(0, part_ref.shape[0] // GROUP, step, 0)


def second_body(given, before, row, skip, final, seg_len, meta_ref, own_ref, part_ref, mark_ref, term_ref, *refs):
    lhs_ref, sem, gate = refs[-3:]
    count, width = part_ref.shape
    chans = own_ref.shape[1]
    outs = []
    if before:
        prior_ref = refs[0]
        out_ref = refs[given]
        target = out_ref.at[pl.ds((row - before) * LAGS, before * LAGS)]
        outs.append(pltpu.make_async_copy(prior_ref, target, sem.at[0]))
        outs[-1].start()
        pl.semaphore_signal(gate, 1)
        pl.semaphore_wait(gate, 1)
    done_ref = refs[-4]
    ending = pl.ds(width - 128, 128)
    here = meta_ref[pl.ds(0, count), :] * mark_ref[pl.ds(0, count), pl.ds(mark_ref.shape[1] - 128, 128)].astype(F32)
    there = own_ref[pl.ds(width + HALF, count), :].astype(F32) * part_ref[:, ending].astype(F32)
    here = here[:, 127:128]
    there = there[:, 127:128]
    scale = 1.0 / (jnp.maximum(here + there, 1.0) * math.sqrt(seg_len))
    here = jnp.broadcast_to(here * scale, (count, chans))
    there = jnp.broadcast_to(there * scale, (count, chans))
    terms = correlate(part_ref[...], own_ref, lhs_ref).astype(BF16).astype(F32)
    slab = 8
    for low in range(0, count, slab):
        at = skip + low
        held_at = at // GROUP * GROUP * HALF + at % GROUP
        for high in range(2):
            lanes = pl.ds(high * chans, chans)
            for first in range(0, HALF, 8):
                tiles = []
                for lag in range(first, first + 8):
                    line = lag * count + low
                    mine = terms[line : line + slab, high * chans : (high + 1) * chans]
                    held = term_ref[pl.ds(held_at + lag * GROUP, slab), lanes].astype(F32)
                    tiles.append(mine * there[low : low + slab] + held * here[low : low + slab])
                turned = jnp.transpose(jnp.stack(tiles, 0), (1, 0, 2))
                for one in range(slab):
                    spot = (low + one) * LAGS + high * HALF + first
                    done_ref[pl.ds(spot, 8), :] = turned[one]
        if final:
            source = done_ref.at[pl.ds(low * LAGS, slab * LAGS)]
            target = out_ref.at[pl.ds((row + low) * LAGS, slab * LAGS)]
            outs.append(pltpu.make_async_copy(source, target, sem.at[1 + low // slab]))
            outs[-1].start()
    for out in outs:
        out.wait()


def body(records, assign, plan, seg_mask):
    chans, seg_count, seg_len = records.shape
    blocks = lax.axis_size("chan")
    half = chans // lax.axis_size("win")
    width = -(-(seg_len + LAGS) // 256) * 256
    win = lax.axis_index("win").astype(jnp.int32).reshape(1)
    rec = records.reshape(chans, seg_count * seg_len).T
    slots = assign.reshape(1, chans)
    nears = [count for side, count in ORDER if side == "near"]
    fars = [count for side, count in ORDER if side == "far"]
    shape = jax.ShapeDtypeStruct
    head = width // 256 * 128
    near_prep = pl.pallas_call(
        near_body,
        out_shape=(
            shape((half, head), BF16),
            shape((head, chans), BF16),
            shape((chans, chans), BF16),
            shape((chans, chans), BF16),
        ),
        in_specs=[SMEM, HBM, HBM],
        out_specs=(VMEM,) * 4,
        scratch_shapes=[
            pltpu.VMEM((chans, chans), F32),
            pltpu.VMEM((1, chans), jnp.int32),
            pltpu.SemaphoreType.DMA((2,)),
        ],
        compiler_params=NEAR_PARAMS,
        cost_estimate=pl.CostEstimate(flops=1 << 26, bytes_accessed=1 << 20, transcendentals=0),
        name="near_prep",
    )
    rest_prep = pl.pallas_call(
        lambda *refs: rest_body(len(nears), *refs),
        out_shape=(shape((width + HALF + 16, chans), BF16), shape((16, 128), F32))
        + tuple(shape((count, width - head), BF16) for count in nears)
        + tuple(shape((count, width), BF16) for count in fars),
        in_specs=[SMEM, HBM] + [VMEM] * 3,
        out_specs=(VMEM,) * (len(ORDER) + 2),
        scratch_shapes=[pltpu.VMEM((width - head, chans), BF16), pltpu.SemaphoreType.DMA((1,))],
        compiler_params=PARAMS,
        cost_estimate=pl.CostEstimate(flops=1 << 27, bytes_accessed=1 << 20, transcendentals=0),
        name="rest_prep",
    )
    rows = GROUP * HALF
    flops = 2 * rows * width * 2 * chans
    lhs = pltpu.VMEM((rows, width), BF16)

    def first(row, *args):
        count = args[2].shape[0]
        return pl.pallas_call(
            lambda *refs: first_body(row, *refs),
            out_shape=shape((count * HALF, 2 * chans), BF16),
            in_specs=[VMEM] * 3 + [ANY] * (len(args) - 3),
            out_specs=VMEM,
            scratch_shapes=[lhs],
            compiler_params=PARAMS,
            cost_estimate=pl.CostEstimate(
                flops=flops * count // GROUP, bytes_accessed=1 << 20, transcendentals=0
            ),
            name="first",
        )(*args)

    def second(before, row, skip, meta, other, part, mark, terms, done, out, after):
        count = part.shape[0]
        final = row + count == half
        total = shape((half * LAGS, chans), F32)
        held = shape((count * LAGS, chans), F32)
        scratch = [
            pltpu.VMEM((count * HALF, width), BF16),
            pltpu.SemaphoreType.DMA((3,)),
            pltpu.SemaphoreType.REGULAR,
        ]
        if final:
            extra = dict(out_shape=(total,), out_specs=(ANY,))
            scratch = [pltpu.VMEM(held.shape, F32)] + scratch
        elif before:
            extra = dict(out_shape=(total, held), out_specs=(ANY, VMEM))
        else:
            extra = dict(out_shape=(held,), out_specs=(VMEM,))
        given = len(done) + len(out) + len(after)
        return pl.pallas_call(
            lambda *refs: second_body(given, before, row, skip, final, seg_len, *refs),
            in_specs=[VMEM] * (5 + len(done)) + [ANY] * (len(out) + len(after)),
            scratch_shapes=scratch,
            input_output_aliases={6: 0} if out else {},
            compiler_params=PARAMS,
            cost_estimate=pl.CostEstimate(
                flops=flops * count // GROUP, bytes_accessed=1 << 20, transcendentals=0
            ),
            name="second",
            **extra,
        )(meta, other, part, mark, terms, *done, *out, *after)

    def exchange(bit):
        straight = []
        crossed = []
        for low in range(blocks):
            for core in range(2):
                straight.append((low * 2 + core, (low ^ 1 << bit) * 2 + core))
                crossed.append((low * 2 + core, (low ^ 1 << bit) * 2 + 1 - core))

        def run(head, pad, turned, pick, rec, flags):
            own, meta, *pieces = rest_prep(flags, rec, pad, turned, pick)
            opening = lax.ppermute(head, ("chan", "win"), straight)
            sent = {"near": pieces[: len(nears)], "far": pieces[len(nears) :]}
            routes = {"near": straight, "far": crossed}
            came = {"near": [], "far": []}
            for at, (side, _) in enumerate(ORDER):
                one = sent[side][len(came[side])]
                came[side].append(lax.ppermute(one, ("chan", "win"), routes[side]))
            other = lax.ppermute(own, "win", [(0, 1), (1, 0)])
            terms = []
            starts = [sum(nears[:at]) for at in range(len(nears))]
            done = out = after = ()
            before = row = taken = 0
            for side, count in ORDER:
                if side == "near":
                    at = len(terms)
                    terms.append(first(starts[at], own, opening, came["near"][at], *after, *done[:1]))
                    after = (terms[-1],)
                    continue
                home = max(at for at in range(len(nears)) if starts[at] <= row)
                after = after[: after != () and after[0] is not terms[home]]
                part = came["far"][taken]
                skip = row - starts[home]
                result = second(before, row, skip, meta, other, part, came["near"][0], terms[home], done, out, after)
                out = result[:1] if before else ()
                done = result[-1:]
                after = ()
                before = count
                row += count
                taken += 1
            return out[0]

        return run

    digits = blocks.bit_length() - 1
    held = near_prep(win, rec, slots)
    branches = [exchange(bit) for bit in range(digits)]
    out = lax.switch(plan[0], branches, *held, rec, seg_mask)
    return jnp.transpose(out.reshape(half, LAGS, chans), (2, 0, 1))[None]


def solution(mesh):
    placed = (P(("days", "chan"), "win", None), P("chan"), P(), P(("days", "chan"), "win"))
    return jax.shard_map(
        body, mesh=mesh, in_specs=placed, out_specs=P("days", "chan", "win", None), check_vma=False
    )
```

time: 30.7 us -> 31.3 us (1.020)
  waiting for transfers between devices: 10.4 us -> 9.09 us
  starting transfers between devices: 6.26 us -> 7.54 us
  Pallas kernels: 12.7 us -> 13.3 us
    ppermute x6 -> x7, waiting for transfers between devices: 10.4 us -> 9.09 us  [the longest x6 9.08 us: run(): came[side].append(lax.ppermute(one, ('chan', 'win'), routes[side]))]
    ppermute x6 -> x7, starting transfers between devices: 5.7 us -> 6.99 us  [the longest x6 4.44 us: run(): came[side].append(lax.ppermute(one, ('chan', 'win'), routes[side]))]
    pallas_call x7, Pallas kernels: 11.2 us -> 12 us  [the longest x4 5.61 us: second(): pl.pallas_call(lambda *refs: second_body(given, before, row, skip, final,...]
  transfers between devices with their start and end apart: 7 -> 8, of which waited for: 3 -> 3; matrix products, arithmetic and copies ran while one was open for 0% -> 0% of each run, Pallas kernels for 26% -> 26%
where the time goes in v2:
time: 31.3 us; the launch traced here: 31.1 us
  Pallas kernels  13.3 us (42%)
  waiting for transfers between devices  9.09 us (29%)
  starting transfers between devices  7.54 us (24%)
  between operations  0.86 us (3%)
  loops' own time  0.36 us (1%)
    ppermute x6, waiting for transfers between devices, run(): came[side].append(lax.ppermute(one, ('chan', 'win'), routes[side]))  9.08 us
    pallas_call x4, Pallas kernels, second(): pl.pallas_call(lambda *refs: second_body(given, before, row, skip, final,...  5.61 us
    ppermute x6, starting transfers between devices, run(): came[side].append(lax.ppermute(one, ('chan', 'win'), routes[side]))  4.44 us
    pallas_call x2, Pallas kernels, first(): pl.pallas_call(lambda *refs: first_body(row, *refs), out_shape=shape((cou...  4.34 us
    ppermute x1, starting transfers between devices, run(): opening = lax.ppermute(head, ('chan', 'win'), straight)  2.55 us
    pallas_call x1, Pallas kernels, run(): own, meta, *pieces = rest_prep(flags, rec, pad, turned, pick)  2.01 us
    pallas_call x1, Pallas kernels, body(): held = near_prep(win, rec, slots)  1.29 us
  transfers between devices with their start and end apart: 8, of which 3 were waited for; matrix products, arithmetic and copies ran while one was open for 0% of the time, Pallas kernels for 26%

profile of v2, /device:TPU:0, one launch (start us, length us, event | category | flops | bytes accessed | tf_op | source)
XLA Modules:
  0.0 31.1 jit_solution(12820695773975008004)
XLA Ops:
  0.7 1.3 %near_prep.1 = (bf16[64,1536]{1,0:T(8,128)(2,1)S(1)}, bf16[1536,128]{1,0:T(8,128)(2,1)S(1)}, bf16[128,128]{1,0:T(8,128)(2,1)S(1)}, bf16[128,128]{1,0:T(8,128)(2,1)S(1)}) custom-call(s32[1]{0:T(128)} %bitcast.3.win_ref, bf16[3000,128]{1,0:T(8,128)(2,1)} %bitcast.11, s32[1,128]{1,0:T(1,128)} %bitcast.15), custom_call_target="tpu_custom_call" | custom-call | flops 67108864 | bytes 1048576 | tf_op jit(solution)/shard_map/near_prep/pallas_call | solution.py:306
  2.0 28.9 %conditional.1 = (f32[4096,128]{1,0:T(8,128)}) conditional(s32[]{:T(128)} %bitcast, (s32[1,1]{1,0:T(1,128)}, bf16[3000,128]{1,0:T(8,128)(2,1)}, bf16[1536,128]{1,0:T(8,128)(2,1)S(1)}, bf16[128,128]{1,0:T(8,128)(2,1)S(1)}, bf16[128,128]{1,0:T(8,128)(2,1)S(1)}, /*index=5*/bf16[64,1536]{1,0:T(8,128)(2,1)S(1)}) %tuple.18, ...), branch_computations={%region_0.0_spmd, %region_1.0_spmd, %region_2.0_spmd} | conditional | flops 6576668672 | bytes 13680968 | solution.py:308
  2.0 2.0 %rest_prep.3 = (bf16[3120,128]{1,0:T(8,128)(2,1)S(1)}, f32[16,128]{1,0:T(8,128)S(1)}, bf16[32,1536]{1,0:T(8,128)(2,1)S(1)}, bf16[32,1536]{1,0:T(8,128)(2,1)S(1)}...) custom-call(s32[1,1]{1,0:T(1,128)} %get-tuple-element.44.refs_0_, ...), custom_call_target="tpu_custom_call" | custom-call | flops 134217728 | bytes 1048576 | tf_op jit(solution)/shard_map/cond/branch_0_fun/rest_prep/pallas_call | solution.py:271
  4.0 0.6 %collective-permute-start = (bf16[3120,128]{1,0:T(8,128)(2,1)S(1)}, bf16[3120,128]{1,0:T(8,128)(2,1)S(1)}, u32[]{:S(2)}, u32[]{:S(2)}) collective-permute-start(bf16[3120,128]{1,0:T(8,128)(2,1)S(1)} %get-tuple-element.51.refs_0_), channel_id=1, source_target_pairs={{0,1},{1,0},{2,3},{3,2},{4,5},{5,4},{6,7},{7,6},{8,9},{9,8},{10,11... | collective-permute-start | bytes 2396168 | tf_op jit(solution)/shard_map/cond/branch_0_fun/ppermute | solution.py:279
  4.5 2.5 %collective-permute-start.3 = (bf16[64,1536]{1,0:T(8,128)(2,1)S(1)}, bf16[64,1536]{1,0:T(8,128)(2,1)S(1)}, u32[]{:S(2)}, u32[]{:S(2)}) collective-permute-start(bf16[64,1536]{1,0:T(8,128)(2,1)S(1)} %get-tuple-element.54), channel_id=1, source_target_pairs={{0,2},{1,3},{2,0},{3,1},{4,6},{5,7},{6,4},{7,5},{8,10},{9,11},{10,... | collective-permute-start | bytes 589832 | tf_op jit(solution)/shard_map/cond/branch_0_fun/ppermute | solution.py:272
  7.1 0.1 collective-permute-start.2
  7.2 1.4 %collective-permute-start.1 = (bf16[16,3072]{1,0:T(8,128)(2,1)S(1)}, bf16[16,3072]{1,0:T(8,128)(2,1)S(1)}, u32[]{:S(2)}, u32[]{:S(2)}) collective-permute-start(bf16[16,3072]{1,0:T(8,128)(2,1)S(1)} %get-tuple-element.52), channel_id=1, source_target_pairs={{0,3},{1,2},{2,1},{3,0},{4,7},{5,6},{6,5},{7,4},{8,11},{9,10},{10,... | collective-permute-start | bytes 294920 | tf_op jit(solution)/shard_map/cond/branch_0_fun/ppermute | solution.py:278
  8.6 0.5 %collective-permute-start.4 = (bf16[32,1536]{1,0:T(8,128)(2,1)S(1)}, bf16[32,1536]{1,0:T(8,128)(2,1)S(1)}, u32[]{:S(2)}, u32[]{:S(2)}) collective-permute-start(bf16[32,1536]{1,0:T(8,128)(2,1)S(1)} %get-tuple-element.55), channel_id=1, source_target_pairs={{0,2},{1,3},{2,0},{3,1},{4,6},{5,7},{6,4},{7,5},{8,10},{9,11},{10,... | collective-permute-start | bytes 294920 | tf_op jit(solution)/shard_map/cond/branch_0_fun/ppermute | solution.py:278
  9.1 5.8 %collective-permute-done.2.refs_2_.refs_3_ = bf16[32,1536]{1,0:T(8,128)(2,1)S(1)} collective-permute-done((bf16[32,1536]{1,0:T(8,128)(2,1)S(1)}, bf16[32,1536]{1,0:T(8,128)(2,1)S(1)}, u32[]{:S(2)}, u32[]{:S(2)}) %collective-permute-start.2) | collective-permute-done | bytes 98336 | tf_op jit(solution)/shard_map/cond/branch_0_fun/ppermute | solution.py:278
  14.9 0.7 %collective-permute-start.5 = (bf16[16,3072]{1,0:T(8,128)(2,1)S(1)}, bf16[16,3072]{1,0:T(8,128)(2,1)S(1)}, u32[]{:S(2)}, u32[]{:S(2)}) collective-permute-start(bf16[16,3072]{1,0:T(8,128)(2,1)S(1)} %get-tuple-element.56), channel_id=1, source_target_pairs={{0,3},{1,2},{2,1},{3,0},{4,7},{5,6},{6,5},{7,4},{8,11},{9,10},{10,... | collective-permute-start | bytes 294920 | tf_op jit(solution)/shard_map/cond/branch_0_fun/ppermute | solution.py:278
  15.6 0.0 collective-permute-done.3.refs_1_
  15.6 1.1 %collective-permute-start.6 = (bf16[16,3072]{1,0:T(8,128)(2,1)S(1)}, bf16[16,3072]{1,0:T(8,128)(2,1)S(1)}, u32[]{:S(2)}, u32[]{:S(2)}) collective-permute-start(bf16[16,3072]{1,0:T(8,128)(2,1)S(1)} %get-tuple-element.57), channel_id=1, source_target_pairs={{0,3},{1,2},{2,1},{3,0},{4,7},{5,6},{6,5},{7,4},{8,11},{9,10},{10,... | collective-permute-start | bytes 294920 | tf_op jit(solution)/shard_map/cond/branch_0_fun/ppermute | solution.py:278
  16.7 2.2 %first.6.refs_3_.refs_4_ = bf16[1024,256]{1,0:T(8,128)(2,1)S(1)} custom-call(bf16[3120,128]{1,0:T(8,128)(2,1)S(1)} %get-tuple-element.51.refs_0_, bf16[64,1536]{1,0:T(8,128)(2,1)S(1)} %collective-permute-done.3.refs_1_, bf16[32,1536]{1,0:T(8,128)(2,1)S(1)} %collective-permute-done.2.refs_2_.refs_3_), custom_call_target="tpu_custom_call" | custom-call | flops 1610612736 | bytes 1048576 | tf_op jit(solution)/shard_map/cond/branch_0_fun/first/pallas_call | solution.py:218
  18.9 0.3 collective-permute-done.4.refs_2_
  19.2 0.7 %collective-permute-start.7 = (bf16[16,3072]{1,0:T(8,128)(2,1)S(1)}, bf16[16,3072]{1,0:T(8,128)(2,1)S(1)}, u32[]{:S(2)}, u32[]{:S(2)}) collective-permute-start(bf16[16,3072]{1,0:T(8,128)(2,1)S(1)} %get-tuple-element.58), channel_id=1, source_target_pairs={{0,3},{1,2},{2,1},{3,0},{4,7},{5,6},{6,5},{7,4},{8,11},{9,10},{10,... | collective-permute-start | bytes 294920 | tf_op jit(solution)/shard_map/cond/branch_0_fun/ppermute | solution.py:278
  19.8 2.2 %first.7.refs_5_.refs_4_ = bf16[1024,256]{1,0:T(8,128)(2,1)S(1)} custom-call(bf16[3120,128]{1,0:T(8,128)(2,1)S(1)} %get-tuple-element.51.refs_0_, bf16[64,1536]{1,0:T(8,128)(2,1)S(1)} %collective-permute-done.3.refs_1_, bf16[32,1536]{1,0:T(8,128)(2,1)S(1)} %collective-permute-done.4.refs_2_, bf16[1024,256]{1,0:T(8,128)(2,1)S(1)} %first.6.refs_3_.refs_4_), custom_call_target="tpu_custom_call" | custom-call | flops 1610612736 | bytes 1048576 | tf_op jit(solution)/shard_map/cond/branch_0_fun/first/pallas_call | solution.py:218
  22.0 3.0 %collective-permute-done.7.refs_2_ = bf16[16,3072]{1,0:T(8,128)(2,1)S(1)} collective-permute-done((bf16[16,3072]{1,0:T(8,128)(2,1)S(1)}, bf16[16,3072]{1,0:T(8,128)(2,1)S(1)}, u32[]{:S(2)}, u32[]{:S(2)}) %collective-permute-start.7) | collective-permute-done | bytes 98336 | tf_op jit(solution)/shard_map/cond/branch_0_fun/ppermute | solution.py:278
  25.0 0.0 collective-permute-done.refs_1_
  25.0 1.2 %second.12.refs_5_ = f32[1024,128]{1,0:T(8,128)S(1)} custom-call(f32[16,128]{1,0:T(8,128)S(1)} %get-tuple-element.50.refs_0_, bf16[3120,128]{1,0:T(8,128)(2,1)S(1)} %collective-permute-done.refs_1_, bf16[16,3072]{1,0:T(8,128)(2,1)S(1)} %collective-permute-done.7.refs_2_, bf16[32,1536]{1,0:T(8,128)(2,1)S(1)} %collective-permute-done.2.refs_2_.refs_3_, ...), custom_call_target="tpu_custom_call" | custom-call | flops 805306368 | bytes 1048576 | tf_op jit(solution)/shard_map/cond/branch_0_fun/second/pallas_call | solution.py:249
  26.2 0.0 collective-permute-done.6.refs_2_
  26.2 1.2 %second.13 = (f32[4096,128]{1,0:T(8,128)}, f32[1024,128]{1,0:T(8,128)S(1)}) custom-call(f32[16,128]{1,0:T(8,128)S(1)} %get-tuple-element.50.refs_0_, bf16[3120,128]{1,0:T(8,128)(2,1)S(1)} %collective-permute-done.refs_1_, bf16[16,3072]{1,0:T(8,128)(2,1)S(1)} %collective-permute-done.6.refs_2_, bf16[32,1536]{1,0:T(8,128)(2,1)S(1)} %collective-permute-done.2.refs_2_.refs_3_, ...), custom_call_target="tpu_custom_call" | custom-call | flops 805306368 | bytes 1048576 | tf_op jit(solution)/shard_map/cond/branch_0_fun/second/pallas_call | solution.py:249
  27.4 0.0 collective-permute-done.5.refs_2_
  27.4 1.2 %second.14 = (f32[4096,128]{1,0:T(8,128)}, f32[1024,128]{1,0:T(8,128)S(1)}) custom-call(f32[16,128]{1,0:T(8,128)S(1)} %get-tuple-element.50.refs_0_, bf16[3120,128]{1,0:T(8,128)(2,1)S(1)} %collective-permute-done.refs_1_, bf16[16,3072]{1,0:T(8,128)(2,1)S(1)} %collective-permute-done.5.refs_2_, ...), custom_call_target="tpu_custom_call", output_to_operand_aliasing={{0}: (6, {})} | custom-call | flops 805306368 | bytes 1048576 | tf_op jit(solution)/shard_map/cond/branch_0_fun/second/pallas_call | solution.py:249
  28.6 0.0 collective-permute-done.1.refs_2_
  28.7 2.0 %second.15 = f32[4096,128]{1,0:T(8,128)} custom-call(f32[16,128]{1,0:T(8,128)S(1)} %get-tuple-element.50.refs_0_, bf16[3120,128]{1,0:T(8,128)(2,1)S(1)} %collective-permute-done.refs_1_, bf16[16,3072]{1,0:T(8,128)(2,1)S(1)} %collective-permute-done.1.refs_2_, ...), custom_call_target="tpu_custom_call", output_to_operand_aliasing={{}: (6, {})} | custom-call | flops 805306368 | bytes 1048576 | tf_op jit(solution)/shard_map/cond/branch_0_fun/second/pallas_call | solution.py:249
Async XLA Ops:
  4.0 21.0 %collective-permute-start = (bf16[3120,128]{1,0:T(8,128)(2,1)S(1)}, bf16[3120,128]{1,0:T(8,128)(2,1)S(1)}, u32[]{:S(2)}, u32[]{:S(2)}) collective-permute-start(bf16[3120,128]{1,0:T(8,128)(2,1)S(1)} %get-tuple-element.51.refs_0_), channel_id=1, source_target_pairs={{0,1},{1,0},{2,3},{3,2},{4,5},{5,4},{6,7},{7,6},{8,9},{9,8},{10,11... | collective-permute-start | bytes 2396168 | tf_op jit(solution)/shard_map/cond/branch_0_fun/ppermute | solution.py:279
  4.5 11.1 %collective-permute-start.3 = (bf16[64,1536]{1,0:T(8,128)(2,1)S(1)}, bf16[64,1536]{1,0:T(8,128)(2,1)S(1)}, u32[]{:S(2)}, u32[]{:S(2)}) collective-permute-start(bf16[64,1536]{1,0:T(8,128)(2,1)S(1)} %get-tuple-element.54), channel_id=1, source_target_pairs={{0,2},{1,3},{2,0},{3,1},{4,6},{5,7},{6,4},{7,5},{8,10},{9,11},{10,... | collective-permute-start | bytes 589832 | tf_op jit(solution)/shard_map/cond/branch_0_fun/ppermute | solution.py:272
  7.1 7.9 %collective-permute-start.2 = (bf16[32,1536]{1,0:T(8,128)(2,1)S(1)}, bf16[32,1536]{1,0:T(8,128)(2,1)S(1)}, u32[]{:S(2)}, u32[]{:S(2)}) collective-permute-start(bf16[32,1536]{1,0:T(8,128)(2,1)S(1)} %get-tuple-element.53), channel_id=1, source_target_pairs={{0,2},{1,3},{2,0},{3,1},{4,6},{5,7},{6,4},{7,5},{8,10},{9,11},{10,... | collective-permute-start | bytes 294920 | tf_op jit(solution)/shard_map/cond/branch_0_fun/ppermute | solution.py:278
  7.2 21.5 %collective-permute-start.1 = (bf16[16,3072]{1,0:T(8,128)(2,1)S(1)}, bf16[16,3072]{1,0:T(8,128)(2,1)S(1)}, u32[]{:S(2)}, u32[]{:S(2)}) collective-permute-start(bf16[16,3072]{1,0:T(8,128)(2,1)S(1)} %get-tuple-element.52), channel_id=1, source_target_pairs={{0,3},{1,2},{2,1},{3,0},{4,7},{5,6},{6,5},{7,4},{8,11},{9,10},{10,... | collective-permute-start | bytes 294920 | tf_op jit(solution)/shard_map/cond/branch_0_fun/ppermute | solution.py:278
  8.6 10.6 %collective-permute-start.4 = (bf16[32,1536]{1,0:T(8,128)(2,1)S(1)}, bf16[32,1536]{1,0:T(8,128)(2,1)S(1)}, u32[]{:S(2)}, u32[]{:S(2)}) collective-permute-start(bf16[32,1536]{1,0:T(8,128)(2,1)S(1)} %get-tuple-element.55), channel_id=1, source_target_pairs={{0,2},{1,3},{2,0},{3,1},{4,6},{5,7},{6,4},{7,5},{8,10},{9,11},{10,... | collective-permute-start | bytes 294920 | tf_op jit(solution)/shard_map/cond/branch_0_fun/ppermute | solution.py:278
  14.9 12.5 %collective-permute-start.5 = (bf16[16,3072]{1,0:T(8,128)(2,1)S(1)}, bf16[16,3072]{1,0:T(8,128)(2,1)S(1)}, u32[]{:S(2)}, u32[]{:S(2)}) collective-permute-start(bf16[16,3072]{1,0:T(8,128)(2,1)S(1)} %get-tuple-element.56), channel_id=1, source_target_pairs={{0,3},{1,2},{2,1},{3,0},{4,7},{5,6},{6,5},{7,4},{8,11},{9,10},{10,... | collective-permute-start | bytes 294920 | tf_op jit(solution)/shard_map/cond/branch_0_fun/ppermute | solution.py:278
  15.6 10.6 %collective-permute-start.6 = (bf16[16,3072]{1,0:T(8,128)(2,1)S(1)}, bf16[16,3072]{1,0:T(8,128)(2,1)S(1)}, u32[]{:S(2)}, u32[]{:S(2)}) collective-permute-start(bf16[16,3072]{1,0:T(8,128)(2,1)S(1)} %get-tuple-element.57), channel_id=1, source_target_pairs={{0,3},{1,2},{2,1},{3,0},{4,7},{5,6},{6,5},{7,4},{8,11},{9,10},{10,... | collective-permute-start | bytes 294920 | tf_op jit(solution)/shard_map/cond/branch_0_fun/ppermute | solution.py:278
  19.2 5.8 %collective-permute-start.7 = (bf16[16,3072]{1,0:T(8,128)(2,1)S(1)}, bf16[16,3072]{1,0:T(8,128)(2,1)S(1)}, u32[]{:S(2)}, u32[]{:S(2)}) collective-permute-start(bf16[16,3072]{1,0:T(8,128)(2,1)S(1)} %get-tuple-element.58), channel_id=1, source_target_pairs={{0,3},{1,2},{2,1},{3,0},{4,7},{5,6},{6,5},{7,4},{8,11},{9,10},{10,... | collective-permute-start | bytes 294920 | tf_op jit(solution)/shard_map/cond/branch_0_fun/ppermute | solution.py:278

commit v3 on v2

--- a/solution.py
+++ b/solution.py
@@ -11,6 +11,7 @@
 LAGS = 64
 HALF = LAGS // 2
 GROUP = 16
+TILE = 128
 ORDER = (('near', 32), ('near', 32), ('far', 16), ('far', 16), ('far', 16), ('far', 16))
 BF16 = jnp.bfloat16
 F32 = jnp.float32
@@ -29,15 +30,13 @@
     ).astype(BF16)
 
 
-def near_body(win_ref, rec_ref, assign_ref, head_ref, pad_ref, rows_ref, pick_ref, turn_ref, slot_ref, sem):
+def near_body(win_ref, rec_ref, assign_ref, head_ref, times_ref, rows_ref, pick_ref, turn_ref, slot_ref, sem):
     chans = rec_ref.shape[1]
     half = chans // 2
-    count = pad_ref.shape[0] - HALF
     slots = pltpu.make_async_copy(assign_ref, slot_ref, sem.at[0])
-    load = pltpu.make_async_copy(rec_ref.at[pl.ds(0, count)], pad_ref.at[pl.ds(HALF, count)], sem.at[1])
+    load = pltpu.make_async_copy(rec_ref.at[pl.ds(0, times_ref.shape[0])], times_ref, sem.at[1])
     slots.start()
     load.start()
-    pad_ref[pl.ds(0, HALF), :] = jnp.zeros((HALF, chans), BF16)
     slots.wait()
     source = lax.broadcasted_iota(jnp.int32, (chans, chans), 0)
     pick = jnp.where(source == slot_ref[...], 1.0, 0.0)
@@ -49,77 +48,92 @@
     rows_ref[pl.ds(0, half), :] = rows
     rows_ref[pl.ds(half, half), :] = turn_ref[pl.ds(far, half), :].astype(BF16)
     load.wait()
-    head_ref[...] = turn(rows, pad_ref)
-
-
-def rest_body(nears, mask_ref, rec_ref, pad_ref, rows_ref, pick_ref, own_ref, meta_ref, *refs):
+    head_ref[...] = turn(rows, times_ref)
+
+
+def rest_body(nears, mask_ref, rec_ref, times_ref, rows_ref, pick_ref, own_ref, meta_ref, *refs):
     out_refs = refs[:-2]
     tail_ref, sem = refs[-2:]
     seg_len, chans = rec_ref.shape
-    head = pad_ref.shape[0]
+    head = times_ref.shape[0]
     rest = tail_ref.shape[0]
     half = chans // 2
-    count = seg_len + HALF - head
+    count = seg_len - head
     load = pltpu.make_async_copy(
-        rec_ref.at[pl.ds(head - HALF, count)], tail_ref.at[pl.ds(0, count)], sem.at[0]
+        rec_ref.at[pl.ds(head, count)], tail_ref.at[pl.ds(0, count)], sem.at[0]
     )
     load.start()
     tail_ref[pl.ds(count, rest - count), :] = jnp.zeros((rest - count, chans), BF16)
     mask = mask_ref[0, 0].astype(F32)
     meta_ref[...] = jnp.full(meta_ref.shape, mask, F32)
-    early = turn(rows_ref[pl.ds(half, half), :], pad_ref)
+    early = turn(rows_ref[pl.ds(half, half), :], times_ref)
     at = 0
     for out_ref in out_refs[nears:]:
         out_ref[:, pl.ds(0, head)] = early[at : at + out_ref.shape[0]]
         at += out_ref.shape[0]
-    own_ref[pl.ds(0, head), :] = jnp.dot(
-        pad_ref[...], pick_ref[...], preferred_element_type=F32
+    own_ref[pl.ds(0, HALF), :] = jnp.zeros((HALF, chans), BF16)
+    own_ref[pl.ds(HALF, head), :] = jnp.dot(
+        times_ref[...], pick_ref[...], preferred_element_type=F32
     ).astype(BF16)
-    own_ref[pl.ds(head + rest, HALF), :] = jnp.zeros((HALF, chans), BF16)
-    own_ref[pl.ds(head + rest + HALF, 16), :] = jnp.full((16, chans), mask, F32).astype(BF16)
+    own_ref[pl.ds(HALF + head + rest, 16), :] = jnp.full((16, chans), mask, F32).astype(BF16)
     load.wait()
     late = turn(rows_ref[...], tail_ref)
-    last = lax.broadcasted_iota(jnp.int32, (chans, 128), 1) == 127
-    ending = jnp.where(last, mask, late[:, rest - 128 :].astype(F32)).astype(BF16)
+    whole = rest - TILE
     at = 0
     for out_ref in out_refs:
         count, width = out_ref.shape
-        out_ref[:, pl.ds(width - rest, rest - 128)] = late[at : at + count, : rest - 128]
-        out_ref[:, pl.ds(width - 128, 128)] = ending[at : at + count]
+        host = width % (2 * TILE) == 0
+        start = width - rest if host else width - whole
+        out_ref[:, pl.ds(start, whole)] = late[at : at + count, :whole]
+        if host:
+            lane = lax.broadcasted_iota(jnp.int32, (count, TILE), 1)
+            mine = late[at : at + count, whole:].astype(F32)
+            guest = pltpu.roll(late[at + count : at + 2 * count, whole:].astype(F32), TILE // 2, 1)
+            ending = jnp.where(lane == TILE - 1, mask, jnp.where(lane < TILE // 2, mine, guest))
+            out_ref[:, pl.ds(width - TILE, TILE)] = ending.astype(BF16)
         at += count
-    own_ref[pl.ds(head, rest), :] = jnp.dot(
+    own_ref[pl.ds(HALF + head, rest), :] = jnp.dot(
         tail_ref[...], pick_ref[...], preferred_element_type=F32
     ).astype(BF16)
 
 
+def ending(tile, guest, left):
+    tile = tile.astype(F32)
+    if guest:
+        tile = pltpu.roll(tile, TILE // 2, 1)
+    lane = lax.broadcasted_iota(jnp.int32, tile.shape, 1)
+    return jnp.where(lane < left, tile, 0.0).astype(BF16)
+
+
 def correlate(part, own_ref, lhs_ref):
     count, width = part.shape
-    pack = GROUP // count
-    if pack == 2:
-        part = jnp.concatenate([part, pltpu.roll(part, width - 1, 1)], axis=0)
-    for lag in range(0, HALF, pack):
-        moved = part if lag == 0 else pltpu.roll(part, width - lag, 1)
-        lhs_ref[pl.ds(lag * count, GROUP), :] = moved
+    for lag in range(HALF):
+        lhs_ref[pl.ds(lag * count, count), :] = pltpu.roll(part, HALF - lag, 1)
     rhs = jnp.concatenate([own_ref[pl.ds(HALF, width), :], own_ref[pl.ds(0, width), :]], axis=1)
     return jnp.dot(lhs_ref[...], rhs, preferred_element_type=F32)
 
 
-def first_body(row, own_ref, head_ref, part_ref, *refs):
+def first_body(row, guest, left, own_ref, head_ref, part_ref, host_ref, *refs):
     term_ref, lhs_ref = refs[-2:]
+    whole = host_ref.shape[1] - TILE
 
     def step(at, carry):
+        rows = pl.ds(pl.multiple_of(at * GROUP, GROUP), GROUP)
         early = head_ref[pl.ds(pl.multiple_of(row + at * GROUP, GROUP), GROUP), :]
-        late = part_ref[pl.ds(pl.multiple_of(at * GROUP, GROUP), GROUP), :]
-        terms = correlate(jnp.concatenate([early, late], axis=1), own_ref, lhs_ref).astype(BF16)
+        last = ending(host_ref[rows, pl.ds(whole, TILE)], guest, left)
+        part = jnp.concatenate([early, part_ref[rows, pl.ds(0, whole)], last], axis=1)
+        terms = correlate(part, own_ref, lhs_ref).astype(BF16)
         term_ref[pl.ds(pl.multiple_of(at * GROUP * HALF, GROUP), GROUP * HALF), :] = terms
         return carry
 
     lax.fori_loop(0, part_ref.shape[0] // GROUP, step, 0)
 
 
-def second_body(given, before, row, skip, final, seg_len, meta_ref, own_ref, part_ref, mark_ref, term_ref, *refs):
+def second_body(
+    given, before, row, skip, guest, final, seg_len, meta_ref, own_ref, part_ref, host_ref, mark_ref, term_ref, *refs
+):
     lhs_ref, sem, gate = refs[-3:]
-    count, width = part_ref.shape
+    count, width = host_ref.shape
     chans = own_ref.shape[1]
     outs = []
     if before:
@@ -131,15 +145,17 @@
         pl.semaphore_signal(gate, 1)
         pl.semaphore_wait(gate, 1)
     done_ref = refs[-4]
-    ending = pl.ds(width - 128, 128)
-    here = meta_ref[pl.ds(0, count), :] * mark_ref[pl.ds(0, count), pl.ds(mark_ref.shape[1] - 128, 128)].astype(F32)
-    there = own_ref[pl.ds(width + HALF, count), :].astype(F32) * part_ref[:, ending].astype(F32)
-    here = here[:, 127:128]
-    there = there[:, 127:128]
+    tile = host_ref[:, pl.ds(width - TILE, TILE)]
+    here = meta_ref[pl.ds(0, count), :] * mark_ref[pl.ds(0, count), pl.ds(mark_ref.shape[1] - TILE, TILE)].astype(F32)
+    there = own_ref[pl.ds(width + HALF, count), :].astype(F32) * tile.astype(F32)
+    here = here[:, TILE - 1 :]
+    there = there[:, TILE - 1 :]
     scale = 1.0 / (jnp.maximum(here + there, 1.0) * math.sqrt(seg_len))
     here = jnp.broadcast_to(here * scale, (count, chans))
     there = jnp.broadcast_to(there * scale, (count, chans))
-    terms = correlate(part_ref[...], own_ref, lhs_ref).astype(BF16).astype(F32)
+    last = ending(tile, guest, seg_len % TILE)
+    part = jnp.concatenate([part_ref[:, pl.ds(0, width - TILE)], last], axis=1)
+    terms = correlate(part, own_ref, lhs_ref).astype(BF16).astype(F32)
     slab = 8
     for low in range(0, count, slab):
         at = skip + low
@@ -170,14 +186,16 @@
     chans, seg_count, seg_len = records.shape
     blocks = lax.axis_size("chan")
     half = chans // lax.axis_size("win")
-    width = -(-(seg_len + LAGS) // 256) * 256
+    width = -(-(seg_len + LAGS) // (2 * TILE)) * 2 * TILE
+    if width - TILE != seg_len // TILE * TILE or seg_len % TILE > TILE // 2:
+        raise ValueError("segment length")
     win = lax.axis_index("win").astype(jnp.int32).reshape(1)
     rec = records.reshape(chans, seg_count * seg_len).T
     slots = assign.reshape(1, chans)
     nears = [count for side, count in ORDER if side == "near"]
     fars = [count for side, count in ORDER if side == "far"]
     shape = jax.ShapeDtypeStruct
-    head = width // 256 * 128
+    head = width // (4 * TILE) * 2 * TILE
     near_prep = pl.pallas_call(
         near_body,
         out_shape=(
@@ -200,8 +218,8 @@
     rest_prep = pl.pallas_call(
         lambda *refs: rest_body(len(nears), *refs),
         out_shape=(shape((width + HALF + 16, chans), BF16), shape((16, 128), F32))
-        + tuple(shape((count, width - head), BF16) for count in nears)
-        + tuple(shape((count, width), BF16) for count in fars),
+        + tuple(shape((count, width - head - at % 2 * TILE), BF16) for at, count in enumerate(nears))
+        + tuple(shape((count, width - at % 2 * TILE), BF16) for at, count in enumerate(fars)),
         in_specs=[SMEM, HBM] + [VMEM] * 3,
         out_specs=(VMEM,) * (len(ORDER) + 2),
         scratch_shapes=[pltpu.VMEM((width - head, chans), BF16), pltpu.SemaphoreType.DMA((1,))],
@@ -213,12 +231,12 @@
     flops = 2 * rows * width * 2 * chans
     lhs = pltpu.VMEM((rows, width), BF16)
 
-    def first(row, *args):
+    def first(row, guest, *args):
         count = args[2].shape[0]
         return pl.pallas_call(
-            lambda *refs: first_body(row, *refs),
+            lambda *refs: first_body(row, guest, seg_len % TILE, *refs),
             out_shape=shape((count * HALF, 2 * chans), BF16),
-            in_specs=[VMEM] * 3 + [ANY] * (len(args) - 3),
+            in_specs=[VMEM] * 4 + [ANY] * (len(args) - 4),
             out_specs=VMEM,
             scratch_shapes=[lhs],
             compiler_params=PARAMS,
@@ -228,7 +246,7 @@
             name="first",
         )(*args)
 
-    def second(before, row, skip, meta, other, part, mark, terms, done, out, after):
+    def second(before, row, skip, guest, meta, other, part, host, mark, terms, done, out, after):
         count = part.shape[0]
         final = row + count == half
         total = shape((half * LAGS, chans), F32)
@@ -247,17 +265,17 @@
             extra = dict(out_shape=(held,), out_specs=(VMEM,))
         given = len(done) + len(out) + len(after)
         return pl.pallas_call(
-            lambda *refs: second_body(given, before, row, skip, final, seg_len, *refs),
-            in_specs=[VMEM] * (5 + len(done)) + [ANY] * (len(out) + len(after)),
+            lambda *refs: second_body(given, before, row, skip, guest, final, seg_len, *refs),
+            in_specs=[VMEM] * (6 + len(done)) + [ANY] * (len(out) + len(after)),
             scratch_shapes=scratch,
-            input_output_aliases={6: 0} if out else {},
+            input_output_aliases={7: 0} if out else {},
             compiler_params=PARAMS,
             cost_estimate=pl.CostEstimate(
                 flops=flops * count // GROUP, bytes_accessed=1 << 20, transcendentals=0
             ),
             name="second",
             **extra,
-        )(meta, other, part, mark, terms, *done, *out, *after)
+        )(meta, other, part, host, mark, terms, *done, *out, *after)
 
     def exchange(bit):
         straight = []
@@ -284,14 +302,19 @@
             for side, count in ORDER:
                 if side == "near":
                     at = len(terms)
-                    terms.append(first(starts[at], own, opening, came["near"][at], *after, *done[:1]))
+                    guest = at % 2
+                    parts = (came["near"][at], came["near"][at - guest])
+                    terms.append(first(starts[at], guest, own, opening, *parts, *after, *done[:1]))
                     after = (terms[-1],)
                     continue
                 home = max(at for at in range(len(nears)) if starts[at] <= row)
                 after = after[: after != () and after[0] is not terms[home]]
-                part = came["far"][taken]
+                guest = taken % 2
+                parts = (came["far"][taken], came["far"][taken - guest])
                 skip = row - starts[home]
-                result = second(before, row, skip, meta, other, part, came["near"][0], terms[home], done, out, after)
+                result = second(
+                    before, row, skip, guest, meta, other, *parts, came["near"][0], terms[home], done, out, after
+                )
                 out = result[:1] if before else ()
                 done = result[-1:]
                 after = ()

time: 31.3 us -> 31.1 us (level)
  waiting for transfers between devices: 9.09 us -> 8.64 us
    ppermute x6, waiting for transfers between devices: 9.08 us -> 8.63 us  [run(): came[side].append(lax.ppermute(one, ('chan', 'win'), routes[side]))]
  transfers between devices with their start and end apart: 8 -> 8, of which waited for: 3 -> 2; matrix products, arithmetic and copies ran while one was open for 0% -> 0% of each run, Pallas kernels for 26% -> 26%
where the time goes in v3:
time: 31.1 us; the launch traced here: 30.9 us
  Pallas kernels  13.4 us (43%)
  waiting for transfers between devices  8.64 us (28%)
  starting transfers between devices  7.61 us (24%)
  between operations  0.86 us (3%)
  loops' own time  0.37 us (1%)
    ppermute x6, waiting for transfers between devices, run(): came[side].append(lax.ppermute(one, ('chan', 'win'), routes[side]))  8.63 us
    pallas_call x4, Pallas kernels, second(): pl.pallas_call(lambda *refs: second_body(given, before, row, skip, guest,...  5.65 us
    ppermute x6, starting transfers between devices, run(): came[side].append(lax.ppermute(one, ('chan', 'win'), routes[side]))  4.5 us
    pallas_call x2, Pallas kernels, first(): pl.pallas_call(lambda *refs: first_body(row, guest, seg_len % TILE, *refs...  4.37 us
    ppermute x1, starting transfers between devices, run(): opening = lax.ppermute(head, ('chan', 'win'), straight)  2.55 us
    pallas_call x1, Pallas kernels, run(): own, meta, *pieces = rest_prep(flags, rec, pad, turned, pick)  2.07 us
    pallas_call x1, Pallas kernels, body(): held = near_prep(win, rec, slots)  1.29 us
  transfers between devices with their start and end apart: 8, of which 2 were waited for; matrix products, arithmetic and copies ran while one was open for 0% of the time, Pallas kernels for 26%

profile of v3, /device:TPU:0, one launch (start us, length us, event | category | flops | bytes accessed | tf_op | source)
XLA Modules:
  0.0 30.9 jit_solution(16909544957484738788)
XLA Ops:
  0.7 1.3 %near_prep.1 = (bf16[64,1536]{1,0:T(8,128)(2,1)S(1)}, bf16[1536,128]{1,0:T(8,128)(2,1)S(1)}, bf16[128,128]{1,0:T(8,128)(2,1)S(1)}, bf16[128,128]{1,0:T(8,128)(2,1)S(1)}) custom-call(s32[1]{0:T(128)} %bitcast.3.win_ref, bf16[3000,128]{1,0:T(8,128)(2,1)} %bitcast.11, s32[1,128]{1,0:T(1,128)} %bitcast.15), custom_call_target="tpu_custom_call" | custom-call | flops 67108864 | bytes 1048576 | tf_op jit(solution)/shard_map/near_prep/pallas_call | solution.py:329
  2.0 28.7 %conditional.1 = (f32[4096,128]{1,0:T(8,128)}) conditional(s32[]{:T(128)} %bitcast, (s32[1,1]{1,0:T(1,128)}, bf16[3000,128]{1,0:T(8,128)(2,1)}, bf16[1536,128]{1,0:T(8,128)(2,1)S(1)}, bf16[128,128]{1,0:T(8,128)(2,1)S(1)}, bf16[128,128]{1,0:T(8,128)(2,1)S(1)}, /*index=5*/bf16[64,1536]{1,0:T(8,128)(2,1)S(1)}) %tuple.18, ...), branch_computations={%region_0.0_spmd, %region_1.0_spmd, %region_2.0_spmd} | conditional | flops 6576668672 | bytes 13615432 | solution.py:331
  2.0 2.1 %rest_prep.3 = (bf16[3120,128]{1,0:T(8,128)(2,1)S(1)}, f32[16,128]{1,0:T(8,128)S(1)}, bf16[32,1536]{1,0:T(8,128)(2,1)S(1)}, bf16[32,1408]{1,0:T(8,128)(2,1)S(1)}...) custom-call(s32[1,1]{1,0:T(1,128)} %get-tuple-element.44.refs_0_, ...), custom_call_target="tpu_custom_call" | custom-call | flops 134217728 | bytes 1048576 | tf_op jit(solution)/shard_map/cond/branch_0_fun/rest_prep/pallas_call | solution.py:289
  4.1 0.6 %collective-permute-start = (bf16[3120,128]{1,0:T(8,128)(2,1)S(1)}, bf16[3120,128]{1,0:T(8,128)(2,1)S(1)}, u32[]{:S(2)}, u32[]{:S(2)}) collective-permute-start(bf16[3120,128]{1,0:T(8,128)(2,1)S(1)} %get-tuple-element.51.refs_0_), channel_id=1, source_target_pairs={{0,1},{1,0},{2,3},{3,2},{4,5},{5,4},{6,7},{7,6},{8,9},{9,8},{10,11... | collective-permute-start | bytes 2396168 | tf_op jit(solution)/shard_map/cond/branch_0_fun/ppermute | solution.py:297
  4.6 2.6 %collective-permute-start.4 = (bf16[64,1536]{1,0:T(8,128)(2,1)S(1)}, bf16[64,1536]{1,0:T(8,128)(2,1)S(1)}, u32[]{:S(2)}, u32[]{:S(2)}) collective-permute-start(bf16[64,1536]{1,0:T(8,128)(2,1)S(1)} %get-tuple-element.55), channel_id=1, source_target_pairs={{0,2},{1,3},{2,0},{3,1},{4,6},{5,7},{6,4},{7,5},{8,10},{9,11},{10,... | collective-permute-start | bytes 589832 | tf_op jit(solution)/shard_map/cond/branch_0_fun/ppermute | solution.py:290
  7.2 0.1 collective-permute-start.3
  7.2 1.9 %collective-permute-start.5 = (bf16[32,1408]{1,0:T(8,128)(2,1)S(1)}, bf16[32,1408]{1,0:T(8,128)(2,1)S(1)}, u32[]{:S(2)}, u32[]{:S(2)}) collective-permute-start(bf16[32,1408]{1,0:T(8,128)(2,1)S(1)} %get-tuple-element.56), channel_id=1, source_target_pairs={{0,2},{1,3},{2,0},{3,1},{4,6},{5,7},{6,4},{7,5},{8,10},{9,11},{10,... | collective-permute-start | bytes 270344 | tf_op jit(solution)/shard_map/cond/branch_0_fun/ppermute | solution.py:296
  9.2 0.0 collective-permute-start.1
  9.2 5.8 %collective-permute-done.3.refs_2_.refs_3_.refs_4_ = bf16[32,1536]{1,0:T(8,128)(2,1)S(1)} collective-permute-done((bf16[32,1536]{1,0:T(8,128)(2,1)S(1)}, bf16[32,1536]{1,0:T(8,128)(2,1)S(1)}, u32[]{:S(2)}, u32[]{:S(2)}) %collective-permute-start.3) | collective-permute-done | bytes 98336 | tf_op jit(solution)/shard_map/cond/branch_0_fun/ppermute | solution.py:296
  15.0 0.7 %collective-permute-start.6 = (bf16[16,2944]{1,0:T(8,128)(2,1)S(1)}, bf16[16,2944]{1,0:T(8,128)(2,1)S(1)}, u32[]{:S(2)}, u32[]{:S(2)}) collective-permute-start(bf16[16,2944]{1,0:T(8,128)(2,1)S(1)} %get-tuple-element.57), channel_id=1, source_target_pairs={{0,3},{1,2},{2,1},{3,0},{4,7},{5,6},{6,5},{7,4},{8,11},{9,10},{10,... | collective-permute-start | bytes 282632 | tf_op jit(solution)/shard_map/cond/branch_0_fun/ppermute | solution.py:296
  15.7 0.0 collective-permute-done.4.refs_1_
  15.7 1.1 %collective-permute-start.2 = (bf16[16,3072]{1,0:T(8,128)(2,1)S(1)}, bf16[16,3072]{1,0:T(8,128)(2,1)S(1)}, u32[]{:S(2)}, u32[]{:S(2)}) collective-permute-start(bf16[16,3072]{1,0:T(8,128)(2,1)S(1)} %get-tuple-element.53), channel_id=1, source_target_pairs={{0,3},{1,2},{2,1},{3,0},{4,7},{5,6},{6,5},{7,4},{8,11},{9,10},{10,... | collective-permute-start | bytes 294920 | tf_op jit(solution)/shard_map/cond/branch_0_fun/ppermute | solution.py:296
  16.8 2.2 %first.6.refs_4_.refs_5_ = bf16[1024,256]{1,0:T(8,128)(2,1)S(1)} custom-call(bf16[3120,128]{1,0:T(8,128)(2,1)S(1)} %get-tuple-element.51.refs_0_, bf16[64,1536]{1,0:T(8,128)(2,1)S(1)} %collective-permute-done.4.refs_1_, bf16[32,1536]{1,0:T(8,128)(2,1)S(1)} %collective-permute-done.3.refs_2_.refs_3_.refs_4_, ...), custom_call_target="tpu_custom_call" | custom-call | flops 1610612736 | bytes 1048576 | tf_op jit(solution)/shard_map/cond/branch_0_fun/first/pallas_call | solution.py:236
  19.0 0.0 collective-permute-done.5.refs_2_
  19.0 0.7 %collective-permute-start.7 = (bf16[16,3072]{1,0:T(8,128)(2,1)S(1)}, bf16[16,3072]{1,0:T(8,128)(2,1)S(1)}, u32[]{:S(2)}, u32[]{:S(2)}) collective-permute-start(bf16[16,3072]{1,0:T(8,128)(2,1)S(1)} %get-tuple-element.58), channel_id=1, source_target_pairs={{0,3},{1,2},{2,1},{3,0},{4,7},{5,6},{6,5},{7,4},{8,11},{9,10},{10,... | collective-permute-start | bytes 294920 | tf_op jit(solution)/shard_map/cond/branch_0_fun/ppermute | solution.py:296
  19.7 2.2 %first.7.refs_6_.refs_5_ = bf16[1024,256]{1,0:T(8,128)(2,1)S(1)} custom-call(bf16[3120,128]{1,0:T(8,128)(2,1)S(1)} %get-tuple-element.51.refs_0_, bf16[64,1536]{1,0:T(8,128)(2,1)S(1)} %collective-permute-done.4.refs_1_, bf16[32,1408]{1,0:T(8,128)(2,1)S(1)} %collective-permute-done.5.refs_2_, ...), custom_call_target="tpu_custom_call" | custom-call | flops 1610612736 | bytes 1048576 | tf_op jit(solution)/shard_map/cond/branch_0_fun/first/pallas_call | solution.py:236
  21.9 2.8 %collective-permute-done.7.refs_2_.refs_3_ = bf16[16,3072]{1,0:T(8,128)(2,1)S(1)} collective-permute-done((bf16[16,3072]{1,0:T(8,128)(2,1)S(1)}, bf16[16,3072]{1,0:T(8,128)(2,1)S(1)}, u32[]{:S(2)}, u32[]{:S(2)}) %collective-permute-start.7) | collective-permute-done | bytes 98336 | tf_op jit(solution)/shard_map/cond/branch_0_fun/ppermute | solution.py:296
  24.7 0.0 collective-permute-done.refs_1_
  24.7 1.2 %second.12.refs_6_ = f32[1024,128]{1,0:T(8,128)S(1)} custom-call(f32[16,128]{1,0:T(8,128)S(1)} %get-tuple-element.50.refs_0_, bf16[3120,128]{1,0:T(8,128)(2,1)S(1)} %collective-permute-done.refs_1_, bf16[16,3072]{1,0:T(8,128)(2,1)S(1)} %collective-permute-done.7.refs_2_.refs_3_, bf16[16,3072]{1,0:T(8,128)(2,1)S(1)} %collective-permute-done.7.refs_2_.refs_3_, ...), custom_call_target="tpu_custom_call" | custom-call | flops 805306368 | bytes 1048576 | tf_op jit(solution)/shard_map/cond/branch_0_fun/second/pallas_call | solution.py:267
  25.9 0.0 collective-permute-done.6.refs_2_
  25.9 1.2 %second.13 = (f32[4096,128]{1,0:T(8,128)}, f32[1024,128]{1,0:T(8,128)S(1)}) custom-call(f32[16,128]{1,0:T(8,128)S(1)} %get-tuple-element.50.refs_0_, bf16[3120,128]{1,0:T(8,128)(2,1)S(1)} %collective-permute-done.refs_1_, bf16[16,2944]{1,0:T(8,128)(2,1)S(1)} %collective-permute-done.6.refs_2_, bf16[16,3072]{1,0:T(8,128)(2,1)S(1)} %collective-permute-done.7.refs_2_.refs_3_, ...), custom_call_target="tpu_custom_call" | custom-call | flops 805306368 | bytes 1048576 | tf_op jit(solution)/shard_map/cond/branch_0_fun/second/pallas_call | solution.py:267
  27.1 0.0 collective-permute-done.2.refs_2_.refs_3_
  27.2 1.2 %second.14 = (f32[4096,128]{1,0:T(8,128)}, f32[1024,128]{1,0:T(8,128)S(1)}) custom-call(f32[16,128]{1,0:T(8,128)S(1)} %get-tuple-element.50.refs_0_, bf16[3120,128]{1,0:T(8,128)(2,1)S(1)} %collective-permute-done.refs_1_, bf16[16,3072]{1,0:T(8,128)(2,1)S(1)} %collective-permute-done.2.refs_2_.refs_3_, ...), custom_call_target="tpu_custom_call", output_to_operand_aliasing={{0}: (7, {})} | custom-call | flops 805306368 | bytes 1048576 | tf_op jit(solution)/shard_map/cond/branch_0_fun/second/pallas_call | solution.py:267
  28.4 0.0 collective-permute-done.1.refs_2_
  28.4 2.0 %second.15 = f32[4096,128]{1,0:T(8,128)} custom-call(f32[16,128]{1,0:T(8,128)S(1)} %get-tuple-element.50.refs_0_, bf16[3120,128]{1,0:T(8,128)(2,1)S(1)} %collective-permute-done.refs_1_, bf16[16,2944]{1,0:T(8,128)(2,1)S(1)} %collective-permute-done.1.refs_2_, ...), custom_call_target="tpu_custom_call", output_to_operand_aliasing={{}: (7, {})} | custom-call | flops 805306368 | bytes 1048576 | tf_op jit(solution)/shard_map/cond/branch_0_fun/second/pallas_call | solution.py:267
Async XLA Ops:
  4.1 20.6 %collective-permute-start = (bf16[3120,128]{1,0:T(8,128)(2,1)S(1)}, bf16[3120,128]{1,0:T(8,128)(2,1)S(1)}, u32[]{:S(2)}, u32[]{:S(2)}) collective-permute-start(bf16[3120,128]{1,0:T(8,128)(2,1)S(1)} %get-tuple-element.51.refs_0_), channel_id=1, source_target_pairs={{0,1},{1,0},{2,3},{3,2},{4,5},{5,4},{6,7},{7,6},{8,9},{9,8},{10,11... | collective-permute-start | bytes 2396168 | tf_op jit(solution)/shard_map/cond/branch_0_fun/ppermute | solution.py:297
  4.6 11.1 %collective-permute-start.4 = (bf16[64,1536]{1,0:T(8,128)(2,1)S(1)}, bf16[64,1536]{1,0:T(8,128)(2,1)S(1)}, u32[]{:S(2)}, u32[]{:S(2)}) collective-permute-start(bf16[64,1536]{1,0:T(8,128)(2,1)S(1)} %get-tuple-element.55), channel_id=1, source_target_pairs={{0,2},{1,3},{2,0},{3,1},{4,6},{5,7},{6,4},{7,5},{8,10},{9,11},{10,... | collective-permute-start | bytes 589832 | tf_op jit(solution)/shard_map/cond/branch_0_fun/ppermute | solution.py:290
  7.2 7.9 %collective-permute-start.3 = (bf16[32,1536]{1,0:T(8,128)(2,1)S(1)}, bf16[32,1536]{1,0:T(8,128)(2,1)S(1)}, u32[]{:S(2)}, u32[]{:S(2)}) collective-permute-start(bf16[32,1536]{1,0:T(8,128)(2,1)S(1)} %get-tuple-element.54), channel_id=1, source_target_pairs={{0,2},{1,3},{2,0},{3,1},{4,6},{5,7},{6,4},{7,5},{8,10},{9,11},{10,... | collective-permute-start | bytes 294920 | tf_op jit(solution)/shard_map/cond/branch_0_fun/ppermute | solution.py:296
  7.2 11.7 %collective-permute-start.5 = (bf16[32,1408]{1,0:T(8,128)(2,1)S(1)}, bf16[32,1408]{1,0:T(8,128)(2,1)S(1)}, u32[]{:S(2)}, u32[]{:S(2)}) collective-permute-start(bf16[32,1408]{1,0:T(8,128)(2,1)S(1)} %get-tuple-element.56), channel_id=1, source_target_pairs={{0,2},{1,3},{2,0},{3,1},{4,6},{5,7},{6,4},{7,5},{8,10},{9,11},{10,... | collective-permute-start | bytes 270344 | tf_op jit(solution)/shard_map/cond/branch_0_fun/ppermute | solution.py:296
  9.2 19.2 %collective-permute-start.1 = (bf16[16,2944]{1,0:T(8,128)(2,1)S(1)}, bf16[16,2944]{1,0:T(8,128)(2,1)S(1)}, u32[]{:S(2)}, u32[]{:S(2)}) collective-permute-start(bf16[16,2944]{1,0:T(8,128)(2,1)S(1)} %get-tuple-element.52), channel_id=1, source_target_pairs={{0,3},{1,2},{2,1},{3,0},{4,7},{5,6},{6,5},{7,4},{8,11},{9,10},{10,... | collective-permute-start | bytes 282632 | tf_op jit(solution)/shard_map/cond/branch_0_fun/ppermute | solution.py:296
  15.0 10.9 %collective-permute-start.6 = (bf16[16,2944]{1,0:T(8,128)(2,1)S(1)}, bf16[16,2944]{1,0:T(8,128)(2,1)S(1)}, u32[]{:S(2)}, u32[]{:S(2)}) collective-permute-start(bf16[16,2944]{1,0:T(8,128)(2,1)S(1)} %get-tuple-element.57), channel_id=1, source_target_pairs={{0,3},{1,2},{2,1},{3,0},{4,7},{5,6},{6,5},{7,4},{8,11},{9,10},{10,... | collective-permute-start | bytes 282632 | tf_op jit(solution)/shard_map/cond/branch_0_fun/ppermute | solution.py:296
  15.7 11.5 %collective-permute-start.2 = (bf16[16,3072]{1,0:T(8,128)(2,1)S(1)}, bf16[16,3072]{1,0:T(8,128)(2,1)S(1)}, u32[]{:S(2)}, u32[]{:S(2)}) collective-permute-start(bf16[16,3072]{1,0:T(8,128)(2,1)S(1)} %get-tuple-element.53), channel_id=1, source_target_pairs={{0,3},{1,2},{2,1},{3,0},{4,7},{5,6},{6,5},{7,4},{8,11},{9,10},{10,... | collective-permute-start | bytes 294920 | tf_op jit(solution)/shard_map/cond/branch_0_fun/ppermute | solution.py:296
  19.0 5.7 %collective-permute-start.7 = (bf16[16,3072]{1,0:T(8,128)(2,1)S(1)}, bf16[16,3072]{1,0:T(8,128)(2,1)S(1)}, u32[]{:S(2)}, u32[]{:S(2)}) collective-permute-start(bf16[16,3072]{1,0:T(8,128)(2,1)S(1)} %get-tuple-element.58), channel_id=1, source_target_pairs={{0,3},{1,2},{2,1},{3,0},{4,7},{5,6},{6,5},{7,4},{8,11},{9,10},{10,... | collective-permute-start | bytes 294920 | tf_op jit(solution)/shard_map/cond/branch_0_fun/ppermute | solution.py:296

commit v4 on v3

--- a/solution.py
+++ b/solution.py
@@ -52,8 +52,8 @@
 
 
 def rest_body(nears, mask_ref, rec_ref, times_ref, rows_ref, pick_ref, own_ref, meta_ref, *refs):
-    out_refs = refs[:-2]
-    tail_ref, sem = refs[-2:]
+    out_refs = refs[:-3]
+    tail_ref, sem, gate = refs[-3:]
     seg_len, chans = rec_ref.shape
     head = times_ref.shape[0]
     rest = tail_ref.shape[0]
@@ -63,6 +63,8 @@
         rec_ref.at[pl.ds(head, count)], tail_ref.at[pl.ds(0, count)], sem.at[0]
     )
     load.start()
+    pl.semaphore_signal(gate, 1)
+    pl.semaphore_wait(gate, 1)
     tail_ref[pl.ds(count, rest - count), :] = jnp.zeros((rest - count, chans), BF16)
     mask = mask_ref[0, 0].astype(F32)
     meta_ref[...] = jnp.full(meta_ref.shape, mask, F32)
@@ -116,17 +118,10 @@
 def first_body(row, guest, left, own_ref, head_ref, part_ref, host_ref, *refs):
     term_ref, lhs_ref = refs[-2:]
     whole = host_ref.shape[1] - TILE
-
-    def step(at, carry):
-        rows = pl.ds(pl.multiple_of(at * GROUP, GROUP), GROUP)
-        early = head_ref[pl.ds(pl.multiple_of(row + at * GROUP, GROUP), GROUP), :]
-        last = ending(host_ref[rows, pl.ds(whole, TILE)], guest, left)
-        part = jnp.concatenate([early, part_ref[rows, pl.ds(0, whole)], last], axis=1)
-        terms = correlate(part, own_ref, lhs_ref).astype(BF16)
-        term_ref[pl.ds(pl.multiple_of(at * GROUP * HALF, GROUP), GROUP * HALF), :] = terms
-        return carry
-
-    lax.fori_loop(0, part_ref.shape[0] // GROUP, step, 0)
+    count = part_ref.shape[0]
+    last = ending(host_ref[:, pl.ds(whole, TILE)], guest, left)
+    part = jnp.concatenate([head_ref[pl.ds(row, count), :], part_ref[:, pl.ds(0, whole)], last], axis=1)
+    term_ref[...] = correlate(part, own_ref, lhs_ref).astype(BF16)
 
 
 def second_body(
@@ -159,7 +154,7 @@
     slab = 8
     for low in range(0, count, slab):
         at = skip + low
-        held_at = at // GROUP * GROUP * HALF + at % GROUP
+        pace = term_ref.shape[0] // HALF
         for high in range(2):
             lanes = pl.ds(high * chans, chans)
             for first in range(0, HALF, 8):
@@ -167,7 +162,7 @@
                 for lag in range(first, first + 8):
                     line = lag * count + low
                     mine = terms[line : line + slab, high * chans : (high + 1) * chans]
-                    held = term_ref[pl.ds(held_at + lag * GROUP, slab), lanes].astype(F32)
+                    held = term_ref[pl.ds(at + lag * pace, slab), lanes].astype(F32)
                     tiles.append(mine * there[low : low + slab] + held * here[low : low + slab])
                 turned = jnp.transpose(jnp.stack(tiles, 0), (1, 0, 2))
                 for one in range(slab):
@@ -222,7 +217,11 @@
         + tuple(shape((count, width - at % 2 * TILE), BF16) for at, count in enumerate(fars)),
         in_specs=[SMEM, HBM] + [VMEM] * 3,
         out_specs=(VMEM,) * (len(ORDER) + 2),
-        scratch_shapes=[pltpu.VMEM((width - head, chans), BF16), pltpu.SemaphoreType.DMA((1,))],
+        scratch_shapes=[
+            pltpu.VMEM((width - head, chans), BF16),
+            pltpu.SemaphoreType.DMA((1,)),
+            pltpu.SemaphoreType.REGULAR,
+        ],
         compiler_params=PARAMS,
         cost_estimate=pl.CostEstimate(flops=1 << 27, bytes_accessed=1 << 20, transcendentals=0),
         name="rest_prep",
@@ -238,7 +237,7 @@
             out_shape=shape((count * HALF, 2 * chans), BF16),
             in_specs=[VMEM] * 4 + [ANY] * (len(args) - 4),
             out_specs=VMEM,
-            scratch_shapes=[lhs],
+            scratch_shapes=[pltpu.VMEM((count * HALF, width), BF16)],
             compiler_params=PARAMS,
             cost_estimate=pl.CostEstimate(
                 flops=flops * count // GROUP, bytes_accessed=1 << 20, transcendentals=0

time: 31.1 us -> 31.1 us (level)
  waiting for transfers between devices: 8.64 us -> 9.08 us
  Pallas kernels: 13.4 us -> 13 us
    pallas_call x2, Pallas kernels: 4.37 us -> 3.93 us  [first(): pl.pallas_call(lambda *refs: first_body(row, guest, seg_len % TILE, *refs...]
    ppermute x6, waiting for transfers between devices: 8.63 us -> 9.07 us  [run(): came[side].append(lax.ppermute(one, ('chan', 'win'), routes[side]))]
  transfers between devices with their start and end apart: 8 -> 8, of which waited for: 2 -> 2; matrix products, arithmetic and copies ran while one was open for 0% -> 0% of each run, Pallas kernels for 26% -> 25%
where the time goes in v4:
time: 31.1 us; the launch traced here: 30.9 us
  Pallas kernels  13 us (42%)
  waiting for transfers between devices  9.08 us (29%)
  starting transfers between devices  7.61 us (24%)
  between operations  0.86 us (3%)
  loops' own time  0.37 us (1%)
    ppermute x6, waiting for transfers between devices, run(): came[side].append(lax.ppermute(one, ('chan', 'win'), routes[side]))  9.07 us
    pallas_call x4, Pallas kernels, second(): pl.pallas_call(lambda *refs: second_body(given, before, row, skip, guest,...  5.65 us
    ppermute x6, starting transfers between devices, run(): came[side].append(lax.ppermute(one, ('chan', 'win'), routes[side]))  4.5 us
    pallas_call x2, Pallas kernels, first(): pl.pallas_call(lambda *refs: first_body(row, guest, seg_len % TILE, *refs...  3.93 us
    ppermute x1, starting transfers between devices, run(): opening = lax.ppermute(head, ('chan', 'win'), straight)  2.55 us
    pallas_call x1, Pallas kernels, run(): own, meta, *pieces = rest_prep(flags, rec, pad, turned, pick)  2.08 us
    pallas_call x1, Pallas kernels, body(): held = near_prep(win, rec, slots)  1.29 us
  transfers between devices with their start and end apart: 8, of which 2 were waited for; matrix products, arithmetic and copies ran while one was open for 0% of the time, Pallas kernels for 25%

profile of v4, /device:TPU:0, one launch (start us, length us, event | category | flops | bytes accessed | tf_op | source)
XLA Modules:
  0.0 30.9 jit_solution(13218235018621762717)
XLA Ops:
  0.7 1.3 %near_prep.1 = (bf16[64,1536]{1,0:T(8,128)(2,1)S(1)}, bf16[1536,128]{1,0:T(8,128)(2,1)S(1)}, bf16[128,128]{1,0:T(8,128)(2,1)S(1)}, bf16[128,128]{1,0:T(8,128)(2,1)S(1)}) custom-call(s32[1]{0:T(128)} %bitcast.3.win_ref, bf16[3000,128]{1,0:T(8,128)(2,1)} %bitcast.11, s32[1,128]{1,0:T(1,128)} %bitcast.15), custom_call_target="tpu_custom_call" | custom-call | flops 67108864 | bytes 1048576 | tf_op jit(solution)/shard_map/near_prep/pallas_call | solution.py:328
  2.0 28.7 %conditional.1 = (f32[4096,128]{1,0:T(8,128)}) conditional(s32[]{:T(128)} %bitcast, (s32[1,1]{1,0:T(1,128)}, bf16[3000,128]{1,0:T(8,128)(2,1)}, bf16[1536,128]{1,0:T(8,128)(2,1)S(1)}, bf16[128,128]{1,0:T(8,128)(2,1)S(1)}, bf16[128,128]{1,0:T(8,128)(2,1)S(1)}, /*index=5*/bf16[64,1536]{1,0:T(8,128)(2,1)S(1)}) %tuple.18, ...), branch_computations={%region_0.0_spmd, %region_1.0_spmd, %region_2.0_spmd} | conditional | flops 6576668672 | bytes 13615432 | solution.py:330
  2.0 2.1 %rest_prep.3 = (bf16[3120,128]{1,0:T(8,128)(2,1)S(1)}, f32[16,128]{1,0:T(8,128)S(1)}, bf16[32,1536]{1,0:T(8,128)(2,1)S(1)}, bf16[32,1408]{1,0:T(8,128)(2,1)S(1)}...) custom-call(s32[1,1]{1,0:T(1,128)} %get-tuple-element.44.refs_0_, ...), custom_call_target="tpu_custom_call" | custom-call | flops 134217728 | bytes 1048576 | tf_op jit(solution)/shard_map/cond/branch_0_fun/rest_prep/pallas_call | solution.py:288
  4.1 0.6 %collective-permute-start = (bf16[3120,128]{1,0:T(8,128)(2,1)S(1)}, bf16[3120,128]{1,0:T(8,128)(2,1)S(1)}, u32[]{:S(2)}, u32[]{:S(2)}) collective-permute-start(bf16[3120,128]{1,0:T(8,128)(2,1)S(1)} %get-tuple-element.51.refs_0_), channel_id=1, source_target_pairs={{0,1},{1,0},{2,3},{3,2},{4,5},{5,4},{6,7},{7,6},{8,9},{9,8},{10,11... | collective-permute-start | bytes 2396168 | tf_op jit(solution)/shard_map/cond/branch_0_fun/ppermute | solution.py:296
  4.6 2.6 %collective-permute-start.4 = (bf16[64,1536]{1,0:T(8,128)(2,1)S(1)}, bf16[64,1536]{1,0:T(8,128)(2,1)S(1)}, u32[]{:S(2)}, u32[]{:S(2)}) collective-permute-start(bf16[64,1536]{1,0:T(8,128)(2,1)S(1)} %get-tuple-element.55), channel_id=1, source_target_pairs={{0,2},{1,3},{2,0},{3,1},{4,6},{5,7},{6,4},{7,5},{8,10},{9,11},{10,... | collective-permute-start | bytes 589832 | tf_op jit(solution)/shard_map/cond/branch_0_fun/ppermute | solution.py:289
  7.2 0.1 collective-permute-start.3
  7.3 1.9 %collective-permute-start.5 = (bf16[32,1408]{1,0:T(8,128)(2,1)S(1)}, bf16[32,1408]{1,0:T(8,128)(2,1)S(1)}, u32[]{:S(2)}, u32[]{:S(2)}) collective-permute-start(bf16[32,1408]{1,0:T(8,128)(2,1)S(1)} %get-tuple-element.56), channel_id=1, source_target_pairs={{0,2},{1,3},{2,0},{3,1},{4,6},{5,7},{6,4},{7,5},{8,10},{9,11},{10,... | collective-permute-start | bytes 270344 | tf_op jit(solution)/shard_map/cond/branch_0_fun/ppermute | solution.py:295
  9.2 0.0 collective-permute-start.1
  9.2 5.8 %collective-permute-done.3.refs_2_.refs_3_.refs_4_ = bf16[32,1536]{1,0:T(8,128)(2,1)S(1)} collective-permute-done((bf16[32,1536]{1,0:T(8,128)(2,1)S(1)}, bf16[32,1536]{1,0:T(8,128)(2,1)S(1)}, u32[]{:S(2)}, u32[]{:S(2)}) %collective-permute-start.3) | collective-permute-done | bytes 98336 | tf_op jit(solution)/shard_map/cond/branch_0_fun/ppermute | solution.py:295
  15.0 0.7 %collective-permute-start.6 = (bf16[16,2944]{1,0:T(8,128)(2,1)S(1)}, bf16[16,2944]{1,0:T(8,128)(2,1)S(1)}, u32[]{:S(2)}, u32[]{:S(2)}) collective-permute-start(bf16[16,2944]{1,0:T(8,128)(2,1)S(1)} %get-tuple-element.57), channel_id=1, source_target_pairs={{0,3},{1,2},{2,1},{3,0},{4,7},{5,6},{6,5},{7,4},{8,11},{9,10},{10,... | collective-permute-start | bytes 282632 | tf_op jit(solution)/shard_map/cond/branch_0_fun/ppermute | solution.py:295
  15.7 0.0 collective-permute-done.4.refs_1_
  15.7 1.1 %collective-permute-start.2 = (bf16[16,3072]{1,0:T(8,128)(2,1)S(1)}, bf16[16,3072]{1,0:T(8,128)(2,1)S(1)}, u32[]{:S(2)}, u32[]{:S(2)}) collective-permute-start(bf16[16,3072]{1,0:T(8,128)(2,1)S(1)} %get-tuple-element.53), channel_id=1, source_target_pairs={{0,3},{1,2},{2,1},{3,0},{4,7},{5,6},{6,5},{7,4},{8,11},{9,10},{10,... | collective-permute-start | bytes 294920 | tf_op jit(solution)/shard_map/cond/branch_0_fun/ppermute | solution.py:295
  16.8 2.0 %first.6.refs_4_.refs_5_ = bf16[1024,256]{1,0:T(8,128)(2,1)S(1)} custom-call(bf16[3120,128]{1,0:T(8,128)(2,1)S(1)} %get-tuple-element.51.refs_0_, bf16[64,1536]{1,0:T(8,128)(2,1)S(1)} %collective-permute-done.4.refs_1_, bf16[32,1536]{1,0:T(8,128)(2,1)S(1)} %collective-permute-done.3.refs_2_.refs_3_.refs_4_, ...), custom_call_target="tpu_custom_call" | custom-call | flops 1610612736 | bytes 1048576 | tf_op jit(solution)/shard_map/cond/branch_0_fun/first/pallas_call | solution.py:235
  18.7 0.0 collective-permute-done.5.refs_2_
  18.8 0.7 %collective-permute-start.7 = (bf16[16,3072]{1,0:T(8,128)(2,1)S(1)}, bf16[16,3072]{1,0:T(8,128)(2,1)S(1)}, u32[]{:S(2)}, u32[]{:S(2)}) collective-permute-start(bf16[16,3072]{1,0:T(8,128)(2,1)S(1)} %get-tuple-element.58), channel_id=1, source_target_pairs={{0,3},{1,2},{2,1},{3,0},{4,7},{5,6},{6,5},{7,4},{8,11},{9,10},{10,... | collective-permute-start | bytes 294920 | tf_op jit(solution)/shard_map/cond/branch_0_fun/ppermute | solution.py:295
  19.5 2.0 %first.7.refs_6_.refs_5_ = bf16[1024,256]{1,0:T(8,128)(2,1)S(1)} custom-call(bf16[3120,128]{1,0:T(8,128)(2,1)S(1)} %get-tuple-element.51.refs_0_, bf16[64,1536]{1,0:T(8,128)(2,1)S(1)} %collective-permute-done.4.refs_1_, bf16[32,1408]{1,0:T(8,128)(2,1)S(1)} %collective-permute-done.5.refs_2_, ...), custom_call_target="tpu_custom_call" | custom-call | flops 1610612736 | bytes 1048576 | tf_op jit(solution)/shard_map/cond/branch_0_fun/first/pallas_call | solution.py:235
  21.5 3.2 %collective-permute-done.7.refs_2_.refs_3_ = bf16[16,3072]{1,0:T(8,128)(2,1)S(1)} collective-permute-done((bf16[16,3072]{1,0:T(8,128)(2,1)S(1)}, bf16[16,3072]{1,0:T(8,128)(2,1)S(1)}, u32[]{:S(2)}, u32[]{:S(2)}) %collective-permute-start.7) | collective-permute-done | bytes 98336 | tf_op jit(solution)/shard_map/cond/branch_0_fun/ppermute | solution.py:295
  24.7 0.0 collective-permute-done.refs_1_
  24.7 1.2 %second.12.refs_6_ = f32[1024,128]{1,0:T(8,128)S(1)} custom-call(f32[16,128]{1,0:T(8,128)S(1)} %get-tuple-element.50.refs_0_, bf16[3120,128]{1,0:T(8,128)(2,1)S(1)} %collective-permute-done.refs_1_, bf16[16,3072]{1,0:T(8,128)(2,1)S(1)} %collective-permute-done.7.refs_2_.refs_3_, bf16[16,3072]{1,0:T(8,128)(2,1)S(1)} %collective-permute-done.7.refs_2_.refs_3_, ...), custom_call_target="tpu_custom_call" | custom-call | flops 805306368 | bytes 1048576 | tf_op jit(solution)/shard_map/cond/branch_0_fun/second/pallas_call | solution.py:266
  25.9 0.0 collective-permute-done.6.refs_2_
  25.9 1.2 %second.13 = (f32[4096,128]{1,0:T(8,128)}, f32[1024,128]{1,0:T(8,128)S(1)}) custom-call(f32[16,128]{1,0:T(8,128)S(1)} %get-tuple-element.50.refs_0_, bf16[3120,128]{1,0:T(8,128)(2,1)S(1)} %collective-permute-done.refs_1_, bf16[16,2944]{1,0:T(8,128)(2,1)S(1)} %collective-permute-done.6.refs_2_, bf16[16,3072]{1,0:T(8,128)(2,1)S(1)} %collective-permute-done.7.refs_2_.refs_3_, ...), custom_call_target="tpu_custom_call" | custom-call | flops 805306368 | bytes 1048576 | tf_op jit(solution)/shard_map/cond/branch_0_fun/second/pallas_call | solution.py:266
  27.2 0.0 collective-permute-done.2.refs_2_.refs_3_
  27.2 1.2 %second.14 = (f32[4096,128]{1,0:T(8,128)}, f32[1024,128]{1,0:T(8,128)S(1)}) custom-call(f32[16,128]{1,0:T(8,128)S(1)} %get-tuple-element.50.refs_0_, bf16[3120,128]{1,0:T(8,128)(2,1)S(1)} %collective-permute-done.refs_1_, bf16[16,3072]{1,0:T(8,128)(2,1)S(1)} %collective-permute-done.2.refs_2_.refs_3_, ...), custom_call_target="tpu_custom_call", output_to_operand_aliasing={{0}: (7, {})} | custom-call | flops 805306368 | bytes 1048576 | tf_op jit(solution)/shard_map/cond/branch_0_fun/second/pallas_call | solution.py:266
  28.4 0.0 collective-permute-done.1.refs_2_
  28.4 2.0 %second.15 = f32[4096,128]{1,0:T(8,128)} custom-call(f32[16,128]{1,0:T(8,128)S(1)} %get-tuple-element.50.refs_0_, bf16[3120,128]{1,0:T(8,128)(2,1)S(1)} %collective-permute-done.refs_1_, bf16[16,2944]{1,0:T(8,128)(2,1)S(1)} %collective-permute-done.1.refs_2_, ...), custom_call_target="tpu_custom_call", output_to_operand_aliasing={{}: (7, {})} | custom-call | flops 805306368 | bytes 1048576 | tf_op jit(solution)/shard_map/cond/branch_0_fun/second/pallas_call | solution.py:266
Async XLA Ops:
  4.1 20.6 %collective-permute-start = (bf16[3120,128]{1,0:T(8,128)(2,1)S(1)}, bf16[3120,128]{1,0:T(8,128)(2,1)S(1)}, u32[]{:S(2)}, u32[]{:S(2)}) collective-permute-start(bf16[3120,128]{1,0:T(8,128)(2,1)S(1)} %get-tuple-element.51.refs_0_), channel_id=1, source_target_pairs={{0,1},{1,0},{2,3},{3,2},{4,5},{5,4},{6,7},{7,6},{8,9},{9,8},{10,11... | collective-permute-start | bytes 2396168 | tf_op jit(solution)/shard_map/cond/branch_0_fun/ppermute | solution.py:296
  4.6 11.1 %collective-permute-start.4 = (bf16[64,1536]{1,0:T(8,128)(2,1)S(1)}, bf16[64,1536]{1,0:T(8,128)(2,1)S(1)}, u32[]{:S(2)}, u32[]{:S(2)}) collective-permute-start(bf16[64,1536]{1,0:T(8,128)(2,1)S(1)} %get-tuple-element.55), channel_id=1, source_target_pairs={{0,2},{1,3},{2,0},{3,1},{4,6},{5,7},{6,4},{7,5},{8,10},{9,11},{10,... | collective-permute-start | bytes 589832 | tf_op jit(solution)/shard_map/cond/branch_0_fun/ppermute | solution.py:289
  7.2 7.9 %collective-permute-start.3 = (bf16[32,1536]{1,0:T(8,128)(2,1)S(1)}, bf16[32,1536]{1,0:T(8,128)(2,1)S(1)}, u32[]{:S(2)}, u32[]{:S(2)}) collective-permute-start(bf16[32,1536]{1,0:T(8,128)(2,1)S(1)} %get-tuple-element.54), channel_id=1, source_target_pairs={{0,2},{1,3},{2,0},{3,1},{4,6},{5,7},{6,4},{7,5},{8,10},{9,11},{10,... | collective-permute-start | bytes 294920 | tf_op jit(solution)/shard_map/cond/branch_0_fun/ppermute | solution.py:295
  7.3 11.5 %collective-permute-start.5 = (bf16[32,1408]{1,0:T(8,128)(2,1)S(1)}, bf16[32,1408]{1,0:T(8,128)(2,1)S(1)}, u32[]{:S(2)}, u32[]{:S(2)}) collective-permute-start(bf16[32,1408]{1,0:T(8,128)(2,1)S(1)} %get-tuple-element.56), channel_id=1, source_target_pairs={{0,2},{1,3},{2,0},{3,1},{4,6},{5,7},{6,4},{7,5},{8,10},{9,11},{10,... | collective-permute-start | bytes 270344 | tf_op jit(solution)/shard_map/cond/branch_0_fun/ppermute | solution.py:295
  9.2 19.2 %collective-permute-start.1 = (bf16[16,2944]{1,0:T(8,128)(2,1)S(1)}, bf16[16,2944]{1,0:T(8,128)(2,1)S(1)}, u32[]{:S(2)}, u32[]{:S(2)}) collective-permute-start(bf16[16,2944]{1,0:T(8,128)(2,1)S(1)} %get-tuple-element.52), channel_id=1, source_target_pairs={{0,3},{1,2},{2,1},{3,0},{4,7},{5,6},{6,5},{7,4},{8,11},{9,10},{10,... | collective-permute-start | bytes 282632 | tf_op jit(solution)/shard_map/cond/branch_0_fun/ppermute | solution.py:295
  15.0 10.9 %collective-permute-start.6 = (bf16[16,2944]{1,0:T(8,128)(2,1)S(1)}, bf16[16,2944]{1,0:T(8,128)(2,1)S(1)}, u32[]{:S(2)}, u32[]{:S(2)}) collective-permute-start(bf16[16,2944]{1,0:T(8,128)(2,1)S(1)} %get-tuple-element.57), channel_id=1, source_target_pairs={{0,3},{1,2},{2,1},{3,0},{4,7},{5,6},{6,5},{7,4},{8,11},{9,10},{10,... | collective-permute-start | bytes 282632 | tf_op jit(solution)/shard_map/cond/branch_0_fun/ppermute | solution.py:295
  15.7 11.5 %collective-permute-start.2 = (bf16[16,3072]{1,0:T(8,128)(2,1)S(1)}, bf16[16,3072]{1,0:T(8,128)(2,1)S(1)}, u32[]{:S(2)}, u32[]{:S(2)}) collective-permute-start(bf16[16,3072]{1,0:T(8,128)(2,1)S(1)} %get-tuple-element.53), channel_id=1, source_target_pairs={{0,3},{1,2},{2,1},{3,0},{4,7},{5,6},{6,5},{7,4},{8,11},{9,10},{10,... | collective-permute-start | bytes 294920 | tf_op jit(solution)/shard_map/cond/branch_0_fun/ppermute | solution.py:295
  18.8 5.9 %collective-permute-start.7 = (bf16[16,3072]{1,0:T(8,128)(2,1)S(1)}, bf16[16,3072]{1,0:T(8,128)(2,1)S(1)}, u32[]{:S(2)}, u32[]{:S(2)}) collective-permute-start(bf16[16,3072]{1,0:T(8,128)(2,1)S(1)} %get-tuple-element.58), channel_id=1, source_target_pairs={{0,3},{1,2},{2,1},{3,0},{4,7},{5,6},{6,5},{7,4},{8,11},{9,10},{10,... | collective-permute-start | bytes 294920 | tf_op jit(solution)/shard_map/cond/branch_0_fun/ppermute | solution.py:295

commit v5 on v3

--- a/solution.py
+++ b/solution.py
@@ -52,8 +52,8 @@
 
 
 def rest_body(nears, mask_ref, rec_ref, times_ref, rows_ref, pick_ref, own_ref, meta_ref, *refs):
-    out_refs = refs[:-2]
-    tail_ref, sem = refs[-2:]
+    out_refs = refs[:-3]
+    tail_ref, sem, gate = refs[-3:]
     seg_len, chans = rec_ref.shape
     head = times_ref.shape[0]
     rest = tail_ref.shape[0]
@@ -63,6 +63,8 @@
         rec_ref.at[pl.ds(head, count)], tail_ref.at[pl.ds(0, count)], sem.at[0]
     )
     load.start()
+    pl.semaphore_signal(gate, 1)
+    pl.semaphore_wait(gate, 1)
     tail_ref[pl.ds(count, rest - count), :] = jnp.zeros((rest - count, chans), BF16)
     mask = mask_ref[0, 0].astype(F32)
     meta_ref[...] = jnp.full(meta_ref.shape, mask, F32)
@@ -222,7 +224,11 @@
         + tuple(shape((count, width - at % 2 * TILE), BF16) for at, count in enumerate(fars)),
         in_specs=[SMEM, HBM] + [VMEM] * 3,
         out_specs=(VMEM,) * (len(ORDER) + 2),
-        scratch_shapes=[pltpu.VMEM((width - head, chans), BF16), pltpu.SemaphoreType.DMA((1,))],
+        scratch_shapes=[
+            pltpu.VMEM((width - head, chans), BF16),
+            pltpu.SemaphoreType.DMA((1,)),
+            pltpu.SemaphoreType.REGULAR,
+        ],
         compiler_params=PARAMS,
         cost_estimate=pl.CostEstimate(flops=1 << 27, bytes_accessed=1 << 20, transcendentals=0),
         name="rest_prep",

time: 31.1 us -> 31.1 us (level)
  no operation moved by 1% of the time
where the time goes in v5:
time: 31.1 us; the launch traced here: 30.9 us
  Pallas kernels  13.4 us (43%)
  waiting for transfers between devices  8.64 us (28%)
  starting transfers between devices  7.61 us (24%)
  between operations  0.86 us (3%)
  loops' own time  0.37 us (1%)
    ppermute x6, waiting for transfers between devices, run(): came[side].append(lax.ppermute(one, ('chan', 'win'), routes[side]))  8.63 us
    pallas_call x4, Pallas kernels, second(): pl.pallas_call(lambda *refs: second_body(given, before, row, skip, guest,...  5.65 us
    ppermute x6, starting transfers between devices, run(): came[side].append(lax.ppermute(one, ('chan', 'win'), routes[side]))  4.5 us
    pallas_call x2, Pallas kernels, first(): pl.pallas_call(lambda *refs: first_body(row, guest, seg_len % TILE, *refs...  4.37 us
    ppermute x1, starting transfers between devices, run(): opening = lax.ppermute(head, ('chan', 'win'), straight)  2.55 us
    pallas_call x1, Pallas kernels, run(): own, meta, *pieces = rest_prep(flags, rec, pad, turned, pick)  2.08 us
    pallas_call x1, Pallas kernels, body(): held = near_prep(win, rec, slots)  1.29 us
  transfers between devices with their start and end apart: 8, of which 2 were waited for; matrix products, arithmetic and copies ran while one was open for 0% of the time, Pallas kernels for 26%

profile of v5, /device:TPU:0, one launch (start us, length us, event | category | flops | bytes accessed | tf_op | source)
XLA Modules:
  0.0 30.9 jit_solution(10219572422243825116)
XLA Ops:
  0.7 1.3 %near_prep.1 = (bf16[64,1536]{1,0:T(8,128)(2,1)S(1)}, bf16[1536,128]{1,0:T(8,128)(2,1)S(1)}, bf16[128,128]{1,0:T(8,128)(2,1)S(1)}, bf16[128,128]{1,0:T(8,128)(2,1)S(1)}) custom-call(s32[1]{0:T(128)} %bitcast.3.win_ref, bf16[3000,128]{1,0:T(8,128)(2,1)} %bitcast.11, s32[1,128]{1,0:T(1,128)} %bitcast.15), custom_call_target="tpu_custom_call" | custom-call | flops 67108864 | bytes 1048576 | tf_op jit(solution)/shard_map/near_prep/pallas_call | solution.py:335
  2.0 28.7 %conditional.1 = (f32[4096,128]{1,0:T(8,128)}) conditional(s32[]{:T(128)} %bitcast, (s32[1,1]{1,0:T(1,128)}, bf16[3000,128]{1,0:T(8,128)(2,1)}, bf16[1536,128]{1,0:T(8,128)(2,1)S(1)}, bf16[128,128]{1,0:T(8,128)(2,1)S(1)}, bf16[128,128]{1,0:T(8,128)(2,1)S(1)}, /*index=5*/bf16[64,1536]{1,0:T(8,128)(2,1)S(1)}) %tuple.18, ...), branch_computations={%region_0.0_spmd, %region_1.0_spmd, %region_2.0_spmd} | conditional | flops 6576668672 | bytes 13615432 | solution.py:337
  2.0 2.1 %rest_prep.3 = (bf16[3120,128]{1,0:T(8,128)(2,1)S(1)}, f32[16,128]{1,0:T(8,128)S(1)}, bf16[32,1536]{1,0:T(8,128)(2,1)S(1)}, bf16[32,1408]{1,0:T(8,128)(2,1)S(1)}...) custom-call(s32[1,1]{1,0:T(1,128)} %get-tuple-element.44.refs_0_, ...), custom_call_target="tpu_custom_call" | custom-call | flops 134217728 | bytes 1048576 | tf_op jit(solution)/shard_map/cond/branch_0_fun/rest_prep/pallas_call | solution.py:295
  4.1 0.6 %collective-permute-start = (bf16[3120,128]{1,0:T(8,128)(2,1)S(1)}, bf16[3120,128]{1,0:T(8,128)(2,1)S(1)}, u32[]{:S(2)}, u32[]{:S(2)}) collective-permute-start(bf16[3120,128]{1,0:T(8,128)(2,1)S(1)} %get-tuple-element.51.refs_0_), channel_id=1, source_target_pairs={{0,1},{1,0},{2,3},{3,2},{4,5},{5,4},{6,7},{7,6},{8,9},{9,8},{10,11... | collective-permute-start | bytes 2396168 | tf_op jit(solution)/shard_map/cond/branch_0_fun/ppermute | solution.py:303
  4.6 2.6 %collective-permute-start.4 = (bf16[64,1536]{1,0:T(8,128)(2,1)S(1)}, bf16[64,1536]{1,0:T(8,128)(2,1)S(1)}, u32[]{:S(2)}, u32[]{:S(2)}) collective-permute-start(bf16[64,1536]{1,0:T(8,128)(2,1)S(1)} %get-tuple-element.55), channel_id=1, source_target_pairs={{0,2},{1,3},{2,0},{3,1},{4,6},{5,7},{6,4},{7,5},{8,10},{9,11},{10,... | collective-permute-start | bytes 589832 | tf_op jit(solution)/shard_map/cond/branch_0_fun/ppermute | solution.py:296
  7.2 0.1 collective-permute-start.3
  7.3 1.9 %collective-permute-start.5 = (bf16[32,1408]{1,0:T(8,128)(2,1)S(1)}, bf16[32,1408]{1,0:T(8,128)(2,1)S(1)}, u32[]{:S(2)}, u32[]{:S(2)}) collective-permute-start(bf16[32,1408]{1,0:T(8,128)(2,1)S(1)} %get-tuple-element.56), channel_id=1, source_target_pairs={{0,2},{1,3},{2,0},{3,1},{4,6},{5,7},{6,4},{7,5},{8,10},{9,11},{10,... | collective-permute-start | bytes 270344 | tf_op jit(solution)/shard_map/cond/branch_0_fun/ppermute | solution.py:302
  9.2 0.0 collective-permute-start.1
  9.2 5.8 %collective-permute-done.3.refs_2_.refs_3_.refs_4_ = bf16[32,1536]{1,0:T(8,128)(2,1)S(1)} collective-permute-done((bf16[32,1536]{1,0:T(8,128)(2,1)S(1)}, bf16[32,1536]{1,0:T(8,128)(2,1)S(1)}, u32[]{:S(2)}, u32[]{:S(2)}) %collective-permute-start.3) | collective-permute-done | bytes 98336 | tf_op jit(solution)/shard_map/cond/branch_0_fun/ppermute | solution.py:302
  15.0 0.7 %collective-permute-start.6 = (bf16[16,2944]{1,0:T(8,128)(2,1)S(1)}, bf16[16,2944]{1,0:T(8,128)(2,1)S(1)}, u32[]{:S(2)}, u32[]{:S(2)}) collective-permute-start(bf16[16,2944]{1,0:T(8,128)(2,1)S(1)} %get-tuple-element.57), channel_id=1, source_target_pairs={{0,3},{1,2},{2,1},{3,0},{4,7},{5,6},{6,5},{7,4},{8,11},{9,10},{10,... | collective-permute-start | bytes 282632 | tf_op jit(solution)/shard_map/cond/branch_0_fun/ppermute | solution.py:302
  15.7 0.0 collective-permute-done.4.refs_1_
  15.7 1.1 %collective-permute-start.2 = (bf16[16,3072]{1,0:T(8,128)(2,1)S(1)}, bf16[16,3072]{1,0:T(8,128)(2,1)S(1)}, u32[]{:S(2)}, u32[]{:S(2)}) collective-permute-start(bf16[16,3072]{1,0:T(8,128)(2,1)S(1)} %get-tuple-element.53), channel_id=1, source_target_pairs={{0,3},{1,2},{2,1},{3,0},{4,7},{5,6},{6,5},{7,4},{8,11},{9,10},{10,... | collective-permute-start | bytes 294920 | tf_op jit(solution)/shard_map/cond/branch_0_fun/ppermute | solution.py:302
  16.8 2.2 %first.6.refs_4_.refs_5_ = bf16[1024,256]{1,0:T(8,128)(2,1)S(1)} custom-call(bf16[3120,128]{1,0:T(8,128)(2,1)S(1)} %get-tuple-element.51.refs_0_, bf16[64,1536]{1,0:T(8,128)(2,1)S(1)} %collective-permute-done.4.refs_1_, bf16[32,1536]{1,0:T(8,128)(2,1)S(1)} %collective-permute-done.3.refs_2_.refs_3_.refs_4_, ...), custom_call_target="tpu_custom_call" | custom-call | flops 1610612736 | bytes 1048576 | tf_op jit(solution)/shard_map/cond/branch_0_fun/first/pallas_call | solution.py:242
  19.0 0.0 collective-permute-done.5.refs_2_
  19.0 0.7 %collective-permute-start.7 = (bf16[16,3072]{1,0:T(8,128)(2,1)S(1)}, bf16[16,3072]{1,0:T(8,128)(2,1)S(1)}, u32[]{:S(2)}, u32[]{:S(2)}) collective-permute-start(bf16[16,3072]{1,0:T(8,128)(2,1)S(1)} %get-tuple-element.58), channel_id=1, source_target_pairs={{0,3},{1,2},{2,1},{3,0},{4,7},{5,6},{6,5},{7,4},{8,11},{9,10},{10,... | collective-permute-start | bytes 294920 | tf_op jit(solution)/shard_map/cond/branch_0_fun/ppermute | solution.py:302
  19.7 2.2 %first.7.refs_6_.refs_5_ = bf16[1024,256]{1,0:T(8,128)(2,1)S(1)} custom-call(bf16[3120,128]{1,0:T(8,128)(2,1)S(1)} %get-tuple-element.51.refs_0_, bf16[64,1536]{1,0:T(8,128)(2,1)S(1)} %collective-permute-done.4.refs_1_, bf16[32,1408]{1,0:T(8,128)(2,1)S(1)} %collective-permute-done.5.refs_2_, ...), custom_call_target="tpu_custom_call" | custom-call | flops 1610612736 | bytes 1048576 | tf_op jit(solution)/shard_map/cond/branch_0_fun/first/pallas_call | solution.py:242
  21.9 2.8 %collective-permute-done.7.refs_2_.refs_3_ = bf16[16,3072]{1,0:T(8,128)(2,1)S(1)} collective-permute-done((bf16[16,3072]{1,0:T(8,128)(2,1)S(1)}, bf16[16,3072]{1,0:T(8,128)(2,1)S(1)}, u32[]{:S(2)}, u32[]{:S(2)}) %collective-permute-start.7) | collective-permute-done | bytes 98336 | tf_op jit(solution)/shard_map/cond/branch_0_fun/ppermute | solution.py:302
  24.7 0.0 collective-permute-done.refs_1_
  24.7 1.2 %second.12.refs_6_ = f32[1024,128]{1,0:T(8,128)S(1)} custom-call(f32[16,128]{1,0:T(8,128)S(1)} %get-tuple-element.50.refs_0_, bf16[3120,128]{1,0:T(8,128)(2,1)S(1)} %collective-permute-done.refs_1_, bf16[16,3072]{1,0:T(8,128)(2,1)S(1)} %collective-permute-done.7.refs_2_.refs_3_, bf16[16,3072]{1,0:T(8,128)(2,1)S(1)} %collective-permute-done.7.refs_2_.refs_3_, ...), custom_call_target="tpu_custom_call" | custom-call | flops 805306368 | bytes 1048576 | tf_op jit(solution)/shard_map/cond/branch_0_fun/second/pallas_call | solution.py:273
  25.9 0.0 collective-permute-done.6.refs_2_
  25.9 1.2 %second.13 = (f32[4096,128]{1,0:T(8,128)}, f32[1024,128]{1,0:T(8,128)S(1)}) custom-call(f32[16,128]{1,0:T(8,128)S(1)} %get-tuple-element.50.refs_0_, bf16[3120,128]{1,0:T(8,128)(2,1)S(1)} %collective-permute-done.refs_1_, bf16[16,2944]{1,0:T(8,128)(2,1)S(1)} %collective-permute-done.6.refs_2_, bf16[16,3072]{1,0:T(8,128)(2,1)S(1)} %collective-permute-done.7.refs_2_.refs_3_, ...), custom_call_target="tpu_custom_call" | custom-call | flops 805306368 | bytes 1048576 | tf_op jit(solution)/shard_map/cond/branch_0_fun/second/pallas_call | solution.py:273
  27.2 0.0 collective-permute-done.2.refs_2_.refs_3_
  27.2 1.2 %second.14 = (f32[4096,128]{1,0:T(8,128)}, f32[1024,128]{1,0:T(8,128)S(1)}) custom-call(f32[16,128]{1,0:T(8,128)S(1)} %get-tuple-element.50.refs_0_, bf16[3120,128]{1,0:T(8,128)(2,1)S(1)} %collective-permute-done.refs_1_, bf16[16,3072]{1,0:T(8,128)(2,1)S(1)} %collective-permute-done.2.refs_2_.refs_3_, ...), custom_call_target="tpu_custom_call", output_to_operand_aliasing={{0}: (7, {})} | custom-call | flops 805306368 | bytes 1048576 | tf_op jit(solution)/shard_map/cond/branch_0_fun/second/pallas_call | solution.py:273
  28.4 0.0 collective-permute-done.1.refs_2_
  28.4 2.0 %second.15 = f32[4096,128]{1,0:T(8,128)} custom-call(f32[16,128]{1,0:T(8,128)S(1)} %get-tuple-element.50.refs_0_, bf16[3120,128]{1,0:T(8,128)(2,1)S(1)} %collective-permute-done.refs_1_, bf16[16,2944]{1,0:T(8,128)(2,1)S(1)} %collective-permute-done.1.refs_2_, ...), custom_call_target="tpu_custom_call", output_to_operand_aliasing={{}: (7, {})} | custom-call | flops 805306368 | bytes 1048576 | tf_op jit(solution)/shard_map/cond/branch_0_fun/second/pallas_call | solution.py:273
Async XLA Ops:
  4.1 20.6 %collective-permute-start = (bf16[3120,128]{1,0:T(8,128)(2,1)S(1)}, bf16[3120,128]{1,0:T(8,128)(2,1)S(1)}, u32[]{:S(2)}, u32[]{:S(2)}) collective-permute-start(bf16[3120,128]{1,0:T(8,128)(2,1)S(1)} %get-tuple-element.51.refs_0_), channel_id=1, source_target_pairs={{0,1},{1,0},{2,3},{3,2},{4,5},{5,4},{6,7},{7,6},{8,9},{9,8},{10,11... | collective-permute-start | bytes 2396168 | tf_op jit(solution)/shard_map/cond/branch_0_fun/ppermute | solution.py:303
  4.6 11.1 %collective-permute-start.4 = (bf16[64,1536]{1,0:T(8,128)(2,1)S(1)}, bf16[64,1536]{1,0:T(8,128)(2,1)S(1)}, u32[]{:S(2)}, u32[]{:S(2)}) collective-permute-start(bf16[64,1536]{1,0:T(8,128)(2,1)S(1)} %get-tuple-element.55), channel_id=1, source_target_pairs={{0,2},{1,3},{2,0},{3,1},{4,6},{5,7},{6,4},{7,5},{8,10},{9,11},{10,... | collective-permute-start | bytes 589832 | tf_op jit(solution)/shard_map/cond/branch_0_fun/ppermute | solution.py:296
  7.2 7.9 %collective-permute-start.3 = (bf16[32,1536]{1,0:T(8,128)(2,1)S(1)}, bf16[32,1536]{1,0:T(8,128)(2,1)S(1)}, u32[]{:S(2)}, u32[]{:S(2)}) collective-permute-start(bf16[32,1536]{1,0:T(8,128)(2,1)S(1)} %get-tuple-element.54), channel_id=1, source_target_pairs={{0,2},{1,3},{2,0},{3,1},{4,6},{5,7},{6,4},{7,5},{8,10},{9,11},{10,... | collective-permute-start | bytes 294920 | tf_op jit(solution)/shard_map/cond/branch_0_fun/ppermute | solution.py:302
  7.3 11.7 %collective-permute-start.5 = (bf16[32,1408]{1,0:T(8,128)(2,1)S(1)}, bf16[32,1408]{1,0:T(8,128)(2,1)S(1)}, u32[]{:S(2)}, u32[]{:S(2)}) collective-permute-start(bf16[32,1408]{1,0:T(8,128)(2,1)S(1)} %get-tuple-element.56), channel_id=1, source_target_pairs={{0,2},{1,3},{2,0},{3,1},{4,6},{5,7},{6,4},{7,5},{8,10},{9,11},{10,... | collective-permute-start | bytes 270344 | tf_op jit(solution)/shard_map/cond/branch_0_fun/ppermute | solution.py:302
  9.2 19.2 %collective-permute-start.1 = (bf16[16,2944]{1,0:T(8,128)(2,1)S(1)}, bf16[16,2944]{1,0:T(8,128)(2,1)S(1)}, u32[]{:S(2)}, u32[]{:S(2)}) collective-permute-start(bf16[16,2944]{1,0:T(8,128)(2,1)S(1)} %get-tuple-element.52), channel_id=1, source_target_pairs={{0,3},{1,2},{2,1},{3,0},{4,7},{5,6},{6,5},{7,4},{8,11},{9,10},{10,... | collective-permute-start | bytes 282632 | tf_op jit(solution)/shard_map/cond/branch_0_fun/ppermute | solution.py:302
  15.0 10.9 %collective-permute-start.6 = (bf16[16,2944]{1,0:T(8,128)(2,1)S(1)}, bf16[16,2944]{1,0:T(8,128)(2,1)S(1)}, u32[]{:S(2)}, u32[]{:S(2)}) collective-permute-start(bf16[16,2944]{1,0:T(8,128)(2,1)S(1)} %get-tuple-element.57), channel_id=1, source_target_pairs={{0,3},{1,2},{2,1},{3,0},{4,7},{5,6},{6,5},{7,4},{8,11},{9,10},{10,... | collective-permute-start | bytes 282632 | tf_op jit(solution)/shard_map/cond/branch_0_fun/ppermute | solution.py:302
  15.7 11.5 %collective-permute-start.2 = (bf16[16,3072]{1,0:T(8,128)(2,1)S(1)}, bf16[16,3072]{1,0:T(8,128)(2,1)S(1)}, u32[]{:S(2)}, u32[]{:S(2)}) collective-permute-start(bf16[16,3072]{1,0:T(8,128)(2,1)S(1)} %get-tuple-element.53), channel_id=1, source_target_pairs={{0,3},{1,2},{2,1},{3,0},{4,7},{5,6},{6,5},{7,4},{8,11},{9,10},{10,... | collective-permute-start | bytes 294920 | tf_op jit(solution)/shard_map/cond/branch_0_fun/ppermute | solution.py:302
  19.0 5.7 %collective-permute-start.7 = (bf16[16,3072]{1,0:T(8,128)(2,1)S(1)}, bf16[16,3072]{1,0:T(8,128)(2,1)S(1)}, u32[]{:S(2)}, u32[]{:S(2)}) collective-permute-start(bf16[16,3072]{1,0:T(8,128)(2,1)S(1)} %get-tuple-element.58), channel_id=1, source_target_pairs={{0,3},{1,2},{2,1},{3,0},{4,7},{5,6},{6,5},{7,4},{8,11},{9,10},{10,... | collective-permute-start | bytes 294920 | tf_op jit(solution)/shard_map/cond/branch_0_fun/ppermute | solution.py:302

commit v6 on v3

--- a/solution.py
+++ b/solution.py
@@ -132,6 +132,8 @@
 def second_body(
     given, before, row, skip, guest, final, seg_len, meta_ref, own_ref, part_ref, host_ref, mark_ref, term_ref, *refs
 ):
+    if guest:
+        last_ref, *refs = refs
     lhs_ref, sem, gate = refs[-3:]
     count, width = host_ref.shape
     chans = own_ref.shape[1]
@@ -153,7 +155,11 @@
     scale = 1.0 / (jnp.maximum(here + there, 1.0) * math.sqrt(seg_len))
     here = jnp.broadcast_to(here * scale, (count, chans))
     there = jnp.broadcast_to(there * scale, (count, chans))
-    last = ending(tile, guest, seg_len % TILE)
+    if guest:
+        last = last_ref[...]
+    else:
+        last = ending(tile, 0, seg_len % TILE)
+        refs[-5][...] = ending(tile, 1, seg_len % TILE)
     part = jnp.concatenate([part_ref[:, pl.ds(0, width - TILE)], last], axis=1)
     terms = correlate(part, own_ref, lhs_ref).astype(BF16).astype(F32)
     slab = 8
@@ -246,11 +252,13 @@
             name="first",
         )(*args)
 
-    def second(before, row, skip, guest, meta, other, part, host, mark, terms, done, out, after):
+    def second(before, row, skip, last, meta, other, part, host, mark, terms, done, out, after):
         count = part.shape[0]
         final = row + count == half
         total = shape((half * LAGS, chans), F32)
         held = shape((count * LAGS, chans), F32)
+        guest = len(last)
+        ends = () if guest else (shape((count, TILE), BF16),)
         scratch = [
             pltpu.VMEM((count * HALF, width), BF16),
             pltpu.SemaphoreType.DMA((3,)),
@@ -260,22 +268,22 @@
             extra = dict(out_shape=(total,), out_specs=(ANY,))
             scratch = [pltpu.VMEM(held.shape, F32)] + scratch
         elif before:
-            extra = dict(out_shape=(total, held), out_specs=(ANY, VMEM))
+            extra = dict(out_shape=(total, *ends, held), out_specs=(ANY,) + (VMEM,) * (len(ends) + 1))
         else:
-            extra = dict(out_shape=(held,), out_specs=(VMEM,))
+            extra = dict(out_shape=(*ends, held), out_specs=(VMEM,) * (len(ends) + 1))
         given = len(done) + len(out) + len(after)
         return pl.pallas_call(
             lambda *refs: second_body(given, before, row, skip, guest, final, seg_len, *refs),
-            in_specs=[VMEM] * (6 + len(done)) + [ANY] * (len(out) + len(after)),
+            in_specs=[VMEM] * (6 + guest + len(done)) + [ANY] * (len(out) + len(after)),
             scratch_shapes=scratch,
-            input_output_aliases={7: 0} if out else {},
+            input_output_aliases={7 + guest: 0} if out else {},
             compiler_params=PARAMS,
             cost_estimate=pl.CostEstimate(
                 flops=flops * count // GROUP, bytes_accessed=1 << 20, transcendentals=0
             ),
             name="second",
             **extra,
-        )(meta, other, part, host, mark, terms, *done, *out, *after)
+        )(meta, other, part, host, mark, terms, *last, *done, *out, *after)
 
     def exchange(bit):
         straight = []
@@ -297,7 +305,7 @@
             other = lax.ppermute(own, "win", [(0, 1), (1, 0)])
             terms = []
             starts = [sum(nears[:at]) for at in range(len(nears))]
-            done = out = after = ()
+            done = out = after = last = ()
             before = row = taken = 0
             for side, count in ORDER:
                 if side == "near":
@@ -313,10 +321,11 @@
                 parts = (came["far"][taken], came["far"][taken - guest])
                 skip = row - starts[home]
                 result = second(
-                    before, row, skip, guest, meta, other, *parts, came["near"][0], terms[home], done, out, after
+                    before, row, skip, last, meta, other, *parts, came["near"][0], terms[home], done, out, after
                 )
                 out = result[:1] if before else ()
                 done = result[-1:]
+                last = () if guest else result[-2:-1]
                 after = ()
                 before = count
                 row += count

time: 31.1 us -> 31.1 us (level)
  no operation moved by 1% of the time
where the time goes in v6:
time: 31.1 us; the launch traced here: 30.9 us
  Pallas kernels  13.4 us (43%)
  waiting for transfers between devices  8.64 us (28%)
  starting transfers between devices  7.61 us (24%)
  between operations  0.86 us (3%)
  loops' own time  0.37 us (1%)
    ppermute x6, waiting for transfers between devices, run(): came[side].append(lax.ppermute(one, ('chan', 'win'), routes[side]))  8.63 us
    pallas_call x4, Pallas kernels, second(): pl.pallas_call(lambda *refs: second_body(given, before, row, skip, guest,...  5.65 us
    ppermute x6, starting transfers between devices, run(): came[side].append(lax.ppermute(one, ('chan', 'win'), routes[side]))  4.5 us
    pallas_call x2, Pallas kernels, first(): pl.pallas_call(lambda *refs: first_body(row, guest, seg_len % TILE, *refs...  4.37 us
    ppermute x1, starting transfers between devices, run(): opening = lax.ppermute(head, ('chan', 'win'), straight)  2.55 us
    pallas_call x1, Pallas kernels, run(): own, meta, *pieces = rest_prep(flags, rec, pad, turned, pick)  2.07 us
    pallas_call x1, Pallas kernels, body(): held = near_prep(win, rec, slots)  1.29 us
  transfers between devices with their start and end apart: 8, of which 2 were waited for; matrix products, arithmetic and copies ran while one was open for 0% of the time, Pallas kernels for 26%

profile of v6, /device:TPU:0, one launch (start us, length us, event | category | flops | bytes accessed | tf_op | source)
XLA Modules:
  0.0 30.9 jit_solution(2163123258051726710)
XLA Ops:
  0.7 1.3 %near_prep.1 = (bf16[64,1536]{1,0:T(8,128)(2,1)S(1)}, bf16[1536,128]{1,0:T(8,128)(2,1)S(1)}, bf16[128,128]{1,0:T(8,128)(2,1)S(1)}, bf16[128,128]{1,0:T(8,128)(2,1)S(1)}) custom-call(s32[1]{0:T(128)} %bitcast.3.win_ref, bf16[3000,128]{1,0:T(8,128)(2,1)} %bitcast.11, s32[1,128]{1,0:T(1,128)} %bitcast.15), custom_call_target="tpu_custom_call" | custom-call | flops 67108864 | bytes 1048576 | tf_op jit(solution)/shard_map/near_prep/pallas_call | solution.py:338
  2.0 28.7 %conditional.1 = (f32[4096,128]{1,0:T(8,128)}) conditional(s32[]{:T(128)} %bitcast, (s32[1,1]{1,0:T(1,128)}, bf16[3000,128]{1,0:T(8,128)(2,1)}, bf16[1536,128]{1,0:T(8,128)(2,1)S(1)}, bf16[128,128]{1,0:T(8,128)(2,1)S(1)}, bf16[128,128]{1,0:T(8,128)(2,1)S(1)}, /*index=5*/bf16[64,1536]{1,0:T(8,128)(2,1)S(1)}) %tuple.18, ...), branch_computations={%region_0.0_spmd, %region_1.0_spmd, %region_2.0_spmd} | conditional | flops 6576668672 | bytes 13615432 | solution.py:340
  2.0 2.1 %rest_prep.3 = (bf16[3120,128]{1,0:T(8,128)(2,1)S(1)}, f32[16,128]{1,0:T(8,128)S(1)}, bf16[32,1536]{1,0:T(8,128)(2,1)S(1)}, bf16[32,1408]{1,0:T(8,128)(2,1)S(1)}...) custom-call(s32[1,1]{1,0:T(1,128)} %get-tuple-element.44.refs_0_, ...), custom_call_target="tpu_custom_call" | custom-call | flops 134217728 | bytes 1048576 | tf_op jit(solution)/shard_map/cond/branch_0_fun/rest_prep/pallas_call | solution.py:297
  4.1 0.6 %collective-permute-start = (bf16[3120,128]{1,0:T(8,128)(2,1)S(1)}, bf16[3120,128]{1,0:T(8,128)(2,1)S(1)}, u32[]{:S(2)}, u32[]{:S(2)}) collective-permute-start(bf16[3120,128]{1,0:T(8,128)(2,1)S(1)} %get-tuple-element.51.refs_0_), channel_id=1, source_target_pairs={{0,1},{1,0},{2,3},{3,2},{4,5},{5,4},{6,7},{7,6},{8,9},{9,8},{10,11... | collective-permute-start | bytes 2396168 | tf_op jit(solution)/shard_map/cond/branch_0_fun/ppermute | solution.py:305
  4.6 2.6 %collective-permute-start.4 = (bf16[64,1536]{1,0:T(8,128)(2,1)S(1)}, bf16[64,1536]{1,0:T(8,128)(2,1)S(1)}, u32[]{:S(2)}, u32[]{:S(2)}) collective-permute-start(bf16[64,1536]{1,0:T(8,128)(2,1)S(1)} %get-tuple-element.55), channel_id=1, source_target_pairs={{0,2},{1,3},{2,0},{3,1},{4,6},{5,7},{6,4},{7,5},{8,10},{9,11},{10,... | collective-permute-start | bytes 589832 | tf_op jit(solution)/shard_map/cond/branch_0_fun/ppermute | solution.py:298
  7.2 0.1 collective-permute-start.3
  7.2 1.9 %collective-permute-start.5 = (bf16[32,1408]{1,0:T(8,128)(2,1)S(1)}, bf16[32,1408]{1,0:T(8,128)(2,1)S(1)}, u32[]{:S(2)}, u32[]{:S(2)}) collective-permute-start(bf16[32,1408]{1,0:T(8,128)(2,1)S(1)} %get-tuple-element.56), channel_id=1, source_target_pairs={{0,2},{1,3},{2,0},{3,1},{4,6},{5,7},{6,4},{7,5},{8,10},{9,11},{10,... | collective-permute-start | bytes 270344 | tf_op jit(solution)/shard_map/cond/branch_0_fun/ppermute | solution.py:304
  9.2 0.0 collective-permute-start.1
  9.2 5.8 %collective-permute-done.3.refs_2_.refs_3_.refs_4_ = bf16[32,1536]{1,0:T(8,128)(2,1)S(1)} collective-permute-done((bf16[32,1536]{1,0:T(8,128)(2,1)S(1)}, bf16[32,1536]{1,0:T(8,128)(2,1)S(1)}, u32[]{:S(2)}, u32[]{:S(2)}) %collective-permute-start.3) | collective-permute-done | bytes 98336 | tf_op jit(solution)/shard_map/cond/branch_0_fun/ppermute | solution.py:304
  15.0 0.7 %collective-permute-start.6 = (bf16[16,2944]{1,0:T(8,128)(2,1)S(1)}, bf16[16,2944]{1,0:T(8,128)(2,1)S(1)}, u32[]{:S(2)}, u32[]{:S(2)}) collective-permute-start(bf16[16,2944]{1,0:T(8,128)(2,1)S(1)} %get-tuple-element.57), channel_id=1, source_target_pairs={{0,3},{1,2},{2,1},{3,0},{4,7},{5,6},{6,5},{7,4},{8,11},{9,10},{10,... | collective-permute-start | bytes 282632 | tf_op jit(solution)/shard_map/cond/branch_0_fun/ppermute | solution.py:304
  15.7 0.0 collective-permute-done.4.refs_1_
  15.7 1.1 %collective-permute-start.2 = (bf16[16,3072]{1,0:T(8,128)(2,1)S(1)}, bf16[16,3072]{1,0:T(8,128)(2,1)S(1)}, u32[]{:S(2)}, u32[]{:S(2)}) collective-permute-start(bf16[16,3072]{1,0:T(8,128)(2,1)S(1)} %get-tuple-element.53), channel_id=1, source_target_pairs={{0,3},{1,2},{2,1},{3,0},{4,7},{5,6},{6,5},{7,4},{8,11},{9,10},{10,... | collective-permute-start | bytes 294920 | tf_op jit(solution)/shard_map/cond/branch_0_fun/ppermute | solution.py:304
  16.8 2.2 %first.6.refs_4_.refs_5_ = bf16[1024,256]{1,0:T(8,128)(2,1)S(1)} custom-call(bf16[3120,128]{1,0:T(8,128)(2,1)S(1)} %get-tuple-element.51.refs_0_, bf16[64,1536]{1,0:T(8,128)(2,1)S(1)} %collective-permute-done.4.refs_1_, bf16[32,1536]{1,0:T(8,128)(2,1)S(1)} %collective-permute-done.3.refs_2_.refs_3_.refs_4_, ...), custom_call_target="tpu_custom_call" | custom-call | flops 1610612736 | bytes 1048576 | tf_op jit(solution)/shard_map/cond/branch_0_fun/first/pallas_call | solution.py:242
  19.0 0.0 collective-permute-done.5.refs_2_
  19.0 0.7 %collective-permute-start.7 = (bf16[16,3072]{1,0:T(8,128)(2,1)S(1)}, bf16[16,3072]{1,0:T(8,128)(2,1)S(1)}, u32[]{:S(2)}, u32[]{:S(2)}) collective-permute-start(bf16[16,3072]{1,0:T(8,128)(2,1)S(1)} %get-tuple-element.58), channel_id=1, source_target_pairs={{0,3},{1,2},{2,1},{3,0},{4,7},{5,6},{6,5},{7,4},{8,11},{9,10},{10,... | collective-permute-start | bytes 294920 | tf_op jit(solution)/shard_map/cond/branch_0_fun/ppermute | solution.py:304
  19.7 2.2 %first.7.refs_6_.refs_5_ = bf16[1024,256]{1,0:T(8,128)(2,1)S(1)} custom-call(bf16[3120,128]{1,0:T(8,128)(2,1)S(1)} %get-tuple-element.51.refs_0_, bf16[64,1536]{1,0:T(8,128)(2,1)S(1)} %collective-permute-done.4.refs_1_, bf16[32,1408]{1,0:T(8,128)(2,1)S(1)} %collective-permute-done.5.refs_2_, ...), custom_call_target="tpu_custom_call" | custom-call | flops 1610612736 | bytes 1048576 | tf_op jit(solution)/shard_map/cond/branch_0_fun/first/pallas_call | solution.py:242
  21.9 2.8 %collective-permute-done.7.refs_2_.refs_3_ = bf16[16,3072]{1,0:T(8,128)(2,1)S(1)} collective-permute-done((bf16[16,3072]{1,0:T(8,128)(2,1)S(1)}, bf16[16,3072]{1,0:T(8,128)(2,1)S(1)}, u32[]{:S(2)}, u32[]{:S(2)}) %collective-permute-start.7) | collective-permute-done | bytes 98336 | tf_op jit(solution)/shard_map/cond/branch_0_fun/ppermute | solution.py:304
  24.7 0.0 collective-permute-done.refs_1_
  24.7 1.2 %second.12 = (bf16[16,128]{1,0:T(8,128)(2,1)S(1)}, f32[1024,128]{1,0:T(8,128)S(1)}) custom-call(f32[16,128]{1,0:T(8,128)S(1)} %get-tuple-element.50.refs_0_, bf16[3120,128]{1,0:T(8,128)(2,1)S(1)} %collective-permute-done.refs_1_, bf16[16,3072]{1,0:T(8,128)(2,1)S(1)} %collective-permute-done.7.refs_2_.refs_3_, ...), custom_call_target="tpu_custom_call" | custom-call | flops 805306368 | bytes 1048576 | tf_op jit(solution)/shard_map/cond/branch_0_fun/second/pallas_call | solution.py:275
  25.9 0.0 collective-permute-done.6.refs_2_
  25.9 1.2 %second.13 = (f32[4096,128]{1,0:T(8,128)}, f32[1024,128]{1,0:T(8,128)S(1)}) custom-call(f32[16,128]{1,0:T(8,128)S(1)} %get-tuple-element.50.refs_0_, bf16[3120,128]{1,0:T(8,128)(2,1)S(1)} %collective-permute-done.refs_1_, bf16[16,2944]{1,0:T(8,128)(2,1)S(1)} %collective-permute-done.6.refs_2_, bf16[16,3072]{1,0:T(8,128)(2,1)S(1)} %collective-permute-done.7.refs_2_.refs_3_, ...), custom_call_target="tpu_custom_call" | custom-call | flops 805306368 | bytes 1048576 | tf_op jit(solution)/shard_map/cond/branch_0_fun/second/pallas_call | solution.py:275
  27.1 0.0 collective-permute-done.2.refs_2_.refs_3_
  27.2 1.2 %second.14 = (f32[4096,128]{1,0:T(8,128)}, bf16[16,128]{1,0:T(8,128)(2,1)S(1)}, f32[1024,128]{1,0:T(8,128)S(1)}) custom-call(f32[16,128]{1,0:T(8,128)S(1)} %get-tuple-element.50.refs_0_, bf16[3120,128]{1,0:T(8,128)(2,1)S(1)} %collective-permute-done.refs_1_, ...), custom_call_target="tpu_custom_call", output_to_operand_aliasing={{0}: (7, {})} | custom-call | flops 805306368 | bytes 1048576 | tf_op jit(solution)/shard_map/cond/branch_0_fun/second/pallas_call | solution.py:275
  28.4 0.0 collective-permute-done.1.refs_2_
  28.4 2.0 %second.15 = f32[4096,128]{1,0:T(8,128)} custom-call(f32[16,128]{1,0:T(8,128)S(1)} %get-tuple-element.50.refs_0_, bf16[3120,128]{1,0:T(8,128)(2,1)S(1)} %collective-permute-done.refs_1_, bf16[16,2944]{1,0:T(8,128)(2,1)S(1)} %collective-permute-done.1.refs_2_, ...), custom_call_target="tpu_custom_call", output_to_operand_aliasing={{}: (8, {})} | custom-call | flops 805306368 | bytes 1048576 | tf_op jit(solution)/shard_map/cond/branch_0_fun/second/pallas_call | solution.py:275
Async XLA Ops:
  4.1 20.6 %collective-permute-start = (bf16[3120,128]{1,0:T(8,128)(2,1)S(1)}, bf16[3120,128]{1,0:T(8,128)(2,1)S(1)}, u32[]{:S(2)}, u32[]{:S(2)}) collective-permute-start(bf16[3120,128]{1,0:T(8,128)(2,1)S(1)} %get-tuple-element.51.refs_0_), channel_id=1, source_target_pairs={{0,1},{1,0},{2,3},{3,2},{4,5},{5,4},{6,7},{7,6},{8,9},{9,8},{10,11... | collective-permute-start | bytes 2396168 | tf_op jit(solution)/shard_map/cond/branch_0_fun/ppermute | solution.py:305
  4.6 11.1 %collective-permute-start.4 = (bf16[64,1536]{1,0:T(8,128)(2,1)S(1)}, bf16[64,1536]{1,0:T(8,128)(2,1)S(1)}, u32[]{:S(2)}, u32[]{:S(2)}) collective-permute-start(bf16[64,1536]{1,0:T(8,128)(2,1)S(1)} %get-tuple-element.55), channel_id=1, source_target_pairs={{0,2},{1,3},{2,0},{3,1},{4,6},{5,7},{6,4},{7,5},{8,10},{9,11},{10,... | collective-permute-start | bytes 589832 | tf_op jit(solution)/shard_map/cond/branch_0_fun/ppermute | solution.py:298
  7.2 7.9 %collective-permute-start.3 = (bf16[32,1536]{1,0:T(8,128)(2,1)S(1)}, bf16[32,1536]{1,0:T(8,128)(2,1)S(1)}, u32[]{:S(2)}, u32[]{:S(2)}) collective-permute-start(bf16[32,1536]{1,0:T(8,128)(2,1)S(1)} %get-tuple-element.54), channel_id=1, source_target_pairs={{0,2},{1,3},{2,0},{3,1},{4,6},{5,7},{6,4},{7,5},{8,10},{9,11},{10,... | collective-permute-start | bytes 294920 | tf_op jit(solution)/shard_map/cond/branch_0_fun/ppermute | solution.py:304
  7.2 11.7 %collective-permute-start.5 = (bf16[32,1408]{1,0:T(8,128)(2,1)S(1)}, bf16[32,1408]{1,0:T(8,128)(2,1)S(1)}, u32[]{:S(2)}, u32[]{:S(2)}) collective-permute-start(bf16[32,1408]{1,0:T(8,128)(2,1)S(1)} %get-tuple-element.56), channel_id=1, source_target_pairs={{0,2},{1,3},{2,0},{3,1},{4,6},{5,7},{6,4},{7,5},{8,10},{9,11},{10,... | collective-permute-start | bytes 270344 | tf_op jit(solution)/shard_map/cond/branch_0_fun/ppermute | solution.py:304
  9.2 19.2 %collective-permute-start.1 = (bf16[16,2944]{1,0:T(8,128)(2,1)S(1)}, bf16[16,2944]{1,0:T(8,128)(2,1)S(1)}, u32[]{:S(2)}, u32[]{:S(2)}) collective-permute-start(bf16[16,2944]{1,0:T(8,128)(2,1)S(1)} %get-tuple-element.52), channel_id=1, source_target_pairs={{0,3},{1,2},{2,1},{3,0},{4,7},{5,6},{6,5},{7,4},{8,11},{9,10},{10,... | collective-permute-start | bytes 282632 | tf_op jit(solution)/shard_map/cond/branch_0_fun/ppermute | solution.py:304
  15.0 10.9 %collective-permute-start.6 = (bf16[16,2944]{1,0:T(8,128)(2,1)S(1)}, bf16[16,2944]{1,0:T(8,128)(2,1)S(1)}, u32[]{:S(2)}, u32[]{:S(2)}) collective-permute-start(bf16[16,2944]{1,0:T(8,128)(2,1)S(1)} %get-tuple-element.57), channel_id=1, source_target_pairs={{0,3},{1,2},{2,1},{3,0},{4,7},{5,6},{6,5},{7,4},{8,11},{9,10},{10,... | collective-permute-start | bytes 282632 | tf_op jit(solution)/shard_map/cond/branch_0_fun/ppermute | solution.py:304
  15.7 11.5 %collective-permute-start.2 = (bf16[16,3072]{1,0:T(8,128)(2,1)S(1)}, bf16[16,3072]{1,0:T(8,128)(2,1)S(1)}, u32[]{:S(2)}, u32[]{:S(2)}) collective-permute-start(bf16[16,3072]{1,0:T(8,128)(2,1)S(1)} %get-tuple-element.53), channel_id=1, source_target_pairs={{0,3},{1,2},{2,1},{3,0},{4,7},{5,6},{6,5},{7,4},{8,11},{9,10},{10,... | collective-permute-start | bytes 294920 | tf_op jit(solution)/shard_map/cond/branch_0_fun/ppermute | solution.py:304
  19.0 5.7 %collective-permute-start.7 = (bf16[16,3072]{1,0:T(8,128)(2,1)S(1)}, bf16[16,3072]{1,0:T(8,128)(2,1)S(1)}, u32[]{:S(2)}, u32[]{:S(2)}) collective-permute-start(bf16[16,3072]{1,0:T(8,128)(2,1)S(1)} %get-tuple-element.58), channel_id=1, source_target_pairs={{0,3},{1,2},{2,1},{3,0},{4,7},{5,6},{6,5},{7,4},{8,11},{9,10},{10,... | collective-permute-start | bytes 294920 | tf_op jit(solution)/shard_map/cond/branch_0_fun/ppermute | solution.py:304
